TPU v7x, 512 devices: a whole 4x4x16 slice. The times are simulated.
512 devices in a mesh: gx: 32 (over z, core), gy: 16 (over y, x).
Axes of the slice: x: 4, y: 4, z: 16, core: 2. Of those that a mesh axis runs over, the one named last changes fastest.
Arguments:
- start_field: float32 [16, 512, 4096], P(None, 'gx', 'gy'), may hold values from -6 to 6
- classes: int32 [512, 4096], P('gx', 'gy'), may hold values from 0 to 7
- conductor: int32 [512, 4096], P('gx', 'gy'), may hold values from 0 to 15
- drive: float32 [512, 4096], P('gx', 'gy'), may hold values from -6 to 6
- perm_table: float32 [8], replicated, may hold values from 1 to 4
- leaf_x: float32 [512, 4096], P('gx', 'gy'), may hold values from -1.5 to 1.5
- leaf_y: float32 [512, 4096], P('gx', 'gy'), may hold values from -1.5 to 1.5
- fwd_x: float32 [8192, 4096], P('gx', 'gy'), may hold values from -1 to 1
- back_x: float32 [8192, 4096], P('gx', 'gy'), may hold values from -1 to 1
- couple_x: float32 [8192, 4096], P('gx', 'gy'), may hold values from -0.375 to 0.375
- fwd_y: float32 [8192, 4096], P('gx', 'gy'), may hold values from -1 to 1
- back_y: float32 [8192, 4096], P('gx', 'gy'), may hold values from -1 to 1
- couple_y: float32 [8192, 4096], P('gx', 'gy'), may hold values from -0.375 to 0.375
Outputs:
- solved_field: float32 [16, 512, 4096], P(None, 'gx', 'gy')
All inputs are finite; a program needn't handle non-finite values.
Results may differ from a plain program's by a relative error of at most 0.00012.
Values sent between devices are 32-bit elements; how exact they have to be, the bound alone decides.
A program may use at most 128 MiB of HBM per device.

v0:
```python
import jax
import jax.numpy as jnp
from jax import lax
from jax.sharding import PartitionSpec as P

Z = 16


HIGHEST_MODE = lax.Precision.HIGHEST


def with_halo(block, sides, width):
    for axis, dim in sides:
        count = lax.axis_size(axis)
        forward = [(i, i + 1) for i in range(count - 1)]
        backward = [(target, source) for source, target in forward]
        low = lax.ppermute(
            lax.slice_in_dim(block, block.shape[dim] - width, None, axis=dim), axis, forward
        )
        high = lax.ppermute(lax.slice_in_dim(block, 0, width, axis=dim), axis, backward)
        block = jnp.concatenate([low, block, high], axis=dim)
    return block


def passed_along(x, axis, by):
    peers = lax.axis_size(axis)
    pairs = [(i, i + by) for i in range(peers) if 0 <= i + by < peers]
    return lax.ppermute(x, axis, pairs)


def apply_map(state, matrix):
    return jnp.dot(state, matrix, precision=HIGHEST_MODE, preferred_element_type=jnp.float32)


def relay_incoming(matrix, source, count, mover):

    def turn(turn_index, carry):
        outgoing, incoming = carry
        incoming = mover(outgoing)
        return (apply_map(incoming, matrix) + source, incoming)

    final_out, final_in = lax.fori_loop(0, count - 1, turn, (source, jnp.zeros_like(source)))
    return final_in


def local(
    start_field,
    classes,
    conductor,
    drive,
    perm_table,
    leaf_x,
    leaf_y,
    fwd_x,
    back_x,
    couple_x,
    fwd_y,
    back_y,
    couple_y,
):
    excites, rows_dev, span_cells = start_field.shape
    col_halo = with_halo(start_field, (("gx", 1),), 1)
    row_halo = with_halo(start_field, (("gy", 2),), Z)
    beside = (
        col_halo[:, 2:, :]
        + col_halo[:, :-2, :]
        + row_halo[:, :, 2 * Z :]
        + row_halo[:, :, : -2 * Z]
    )
    node_index = lax.broadcasted_iota(jnp.int32, (1, 1, span_cells), 2) % Z
    zero_col = jnp.zeros((excites, rows_dev, 1), jnp.float32)
    upper = jnp.where(
        node_index == Z - 1, 0.0, jnp.concatenate([start_field[:, :, 1:], zero_col], axis=2)
    )
    lower = jnp.where(
        node_index == 0, 0.0, jnp.concatenate([zero_col, start_field[:, :, :-1]], axis=2)
    )
    class_ids = jnp.arange(perm_table.shape[0], dtype=jnp.int32)
    permit = jnp.sum(
        jnp.where(classes[None] == class_ids[:, None, None], perm_table[:, None, None], 0.0), axis=0
    )
    excite_ids = jnp.arange(excites, dtype=jnp.int32)
    source = drive[None] * (conductor[None] == excite_ids[:, None, None]).astype(jnp.float32)
    resid = source - (
        permit[None] * (4.0 * start_field - beside) + 2.0 * start_field - (upper + lower)
    )
    src_x = jnp.sum(leaf_x[None] * resid, axis=1)

    def pass_x_fwd(vector):
        return passed_along(vector, "gx", 1)

    incoming = relay_incoming(fwd_x, src_x, lax.axis_size("gx"), pass_x_fwd)
    ahead = apply_map(incoming, fwd_x) + src_x
    feed_x = apply_map(ahead, couple_x)

    def pass_x_back(vector):
        return passed_along(vector, "gx", -1)

    returning = relay_incoming(back_x, feed_x, lax.axis_size("gx"), pass_x_back)
    across = apply_map(returning, back_x) + feed_x
    across_cells = leaf_x[None] * across[:, None, :]
    lifted = resid + across_cells
    src_y = jnp.sum(
        (lifted * leaf_y[None]).reshape(excites, rows_dev, span_cells // Z, Z), axis=2
    ).reshape(excites, rows_dev * Z)

    def pass_y_fwd(vector):
        return passed_along(vector, "gy", 1)

    incoming_y = relay_incoming(fwd_y, src_y, lax.axis_size("gy"), pass_y_fwd)
    ahead_y = apply_map(incoming_y, fwd_y) + src_y
    feed_y = apply_map(ahead_y, couple_y)

    def pass_y_back(vector):
        return passed_along(vector, "gy", -1)

    returning_y = relay_incoming(back_y, feed_y, lax.axis_size("gy"), pass_y_back)
    along = apply_map(returning_y, back_y) + feed_y
    spread = jnp.broadcast_to(
        along.reshape(excites, rows_dev, 1, Z), (excites, rows_dev, span_cells // Z, Z)
    ).reshape(excites, rows_dev, span_cells)
    return start_field + across_cells + leaf_y[None] * spread


def solution(mesh):
    in_specs = (
        P(None, "gx", "gy"),
        P("gx", "gy"),
        P("gx", "gy"),
        P("gx", "gy"),
        P(),
        P("gx", "gy"),
        P("gx", "gy"),
        P("gx", "gy"),
        P("gx", "gy"),
        P("gx", "gy"),
        P("gx", "gy"),
        P("gx", "gy"),
        P("gx", "gy"),
    )
    out_specs = P(None, "gx", "gy")
    return jax.shard_map(local, mesh=mesh, in_specs=in_specs, out_specs=out_specs, check_vma=False)
```

profile of v0, /device:TPU:406, one launch (start us, length us, event | category | flops | bytes accessed | tf_op | source)
XLA Modules:
  0.0 700.6 jit_solution(9758543557000784365)
XLA Ops:
  21.9 212.9 %while.48 = (s32[]{:T(128)}, f32[16,256]{1,0:T(8,128)S(1)}, f32[16,256]{1,0:T(8,128)}, f32[256,256]{1,0:T(8,128)S(1)}, f32[16,256]{1,0:T(8,128)S(1)}, /*index=5*/s32[]{:T(128)}) while((s32[]{:T(128)}, f32[16,256]{1,0:T(8,128)S(1)}, f32[16,256]{1,0:T(8,128)}, f32[256,256]{1,0:T(8,128)S(1)}, f32[16,256]{1,0:T(8,128)S(1)}, ...), condition=%wide.region_3.4_spmd, body=%wide.region_2.3_spmd.sunk | while | flops 12587010 | bytes 442505 | solution.py:42
  236.6 209.8 %while.49 = (s32[]{:T(128)}, f32[16,256]{1,0:T(8,128)S(1)}, f32[16,256]{1,0:T(8,128)}, f32[256,256]{1,0:T(8,128)S(1)}, f32[16,256]{1,0:T(8,128)S(1)}, /*index=5*/s32[]{:T(128)}) while((s32[]{:T(128)}, f32[16,256]{1,0:T(8,128)S(1)}, f32[16,256]{1,0:T(8,128)}, f32[256,256]{1,0:T(8,128)S(1)}, f32[16,256]{1,0:T(8,128)S(1)}, ...), condition=%wide.region_5.6_spmd, body=%wide.region_4.5_spmd.sunk | while | flops 12587010 | bytes 442505 | solution.py:42
  449.3 121.1 %while.50 = (s32[]{:T(128)}, f32[16,256]{1,0:T(8,128)S(1)}, f32[16,256]{1,0:T(8,128)}, f32[256,256]{1,0:T(8,128)S(1)}, f32[16,256]{1,0:T(8,128)S(1)}, /*index=5*/s32[]{:T(128)}) while((s32[]{:T(128)}, f32[16,256]{1,0:T(8,128)S(1)}, f32[16,256]{1,0:T(8,128)}, f32[256,256]{1,0:T(8,128)S(1)}, f32[16,256]{1,0:T(8,128)S(1)}, ...), condition=%wide.region_8.9_spmd, body=%wide.region_7.8_spmd.sunk | while | flops 12587010 | bytes 442505 | solution.py:42
  461.8 6.3 collective-permute-start.2
  470.2 6.3 collective-permute-start.2
  478.5 6.3 collective-permute-start.2
  486.8 6.3 collective-permute-start.2
  495.2 6.3 collective-permute-start.2
  503.5 6.3 collective-permute-start.2
  511.8 6.3 collective-permute-start.2
  520.2 6.3 collective-permute-start.2
  528.5 6.4 collective-permute-start.2
  537.0 6.3 collective-permute-start.2
  545.3 6.3 collective-permute-start.2
  553.7 6.3 collective-permute-start.2
  562.0 6.3 collective-permute-start.2
  572.2 125.5 %while.51 = (s32[]{:T(128)}, f32[16,256]{1,0:T(8,128)S(1)}, f32[16,256]{1,0:T(8,128)}, f32[256,256]{1,0:T(8,128)S(1)}, f32[16,256]{1,0:T(8,128)S(1)}, /*index=5*/s32[]{:T(128)}) while((s32[]{:T(128)}, f32[16,256]{1,0:T(8,128)S(1)}, f32[16,256]{1,0:T(8,128)}, f32[256,256]{1,0:T(8,128)S(1)}, f32[16,256]{1,0:T(8,128)S(1)}, ...), condition=%wide.region_10.11_spmd, body=%wide.region_9.10_spmd.sunk | while | flops 12587010 | bytes 442505 | solution.py:42
  574.1 6.1 collective-permute-done.3
  582.7 5.8 collective-permute-done.3
  591.0 5.8 collective-permute-done.3
  607.7 5.8 collective-permute-done.3
  632.7 6.0 collective-permute-done.3
  649.5 5.8 collective-permute-done.3
  691.2 5.8 collective-permute-done.3
  (494 shorter events, 575.4 us)
Async XLA Ops:
  1.1 16.0 %collective-permute-start.6 = (f32[16,16,16]{2,1,0:T(8,128)S(1)}, f32[16,16,16]{2,1,0:T(8,128)S(1)}, u32[]{:S(2)}, u32[]{:S(2)}) collective-permute-start(f32[16,16,16]{2,1,0:T(8,128)S(1)} %get-tuple-element.157), channel_id=1, source_target_pairs={{1,0},{2,1},{3,2},{4,3},{5,4},{6,5},{7,6},{8,7},{9,8},{10,9},{11,1... | collective-permute-start | bytes 49160 | tf_op jit(solution)/shard_map/ppermute | solution.py:20
  3.9 13.2 %collective-permute-start.7 = (f32[16,16,16]{2,1,0:T(8,128)S(1)}, f32[16,16,16]{2,1,0:T(8,128)S(1)}, u32[]{:S(2)}, u32[]{:S(2)}) collective-permute-start(f32[16,16,16]{2,1,0:T(8,128)S(1)} %get-tuple-element.158), channel_id=1, source_target_pairs={{0,1},{1,2},{2,3},{3,4},{4,5},{5,6},{6,7},{7,8},{8,9},{9,10},{10,1... | collective-permute-start | bytes 49160 | tf_op jit(solution)/shard_map/ppermute | solution.py:17
  461.8 7.7 %collective-permute-start.2 = (f32[16,256]{1,0:T(8,128)S(1)}, f32[16,256]{1,0:T(8,128)S(1)}, u32[]{:S(2)}, u32[]{:S(2)}) collective-permute-start(f32[16,256]{1,0:T(8,128)S(1)} %get-tuple-element.322), channel_id=1, source_target_pairs={{0,1},{1,2},{2,3},{3,4},{4,5},{5,6},{6,7},{7,8},{8,9},{9,10},{10,1... | collective-permute-start | bytes 49160 | tf_op jit(solution)/shard_map/while/body/eval_jaxpr/ppermute | solution.py:28
  470.2 7.7 %collective-permute-start.2 = (f32[16,256]{1,0:T(8,128)S(1)}, f32[16,256]{1,0:T(8,128)S(1)}, u32[]{:S(2)}, u32[]{:S(2)}) collective-permute-start(f32[16,256]{1,0:T(8,128)S(1)} %get-tuple-element.322), channel_id=1, source_target_pairs={{0,1},{1,2},{2,3},{3,4},{4,5},{5,6},{6,7},{7,8},{8,9},{9,10},{10,1... | collective-permute-start | bytes 49160 | tf_op jit(solution)/shard_map/while/body/eval_jaxpr/ppermute | solution.py:28
  478.5 7.7 %collective-permute-start.2 = (f32[16,256]{1,0:T(8,128)S(1)}, f32[16,256]{1,0:T(8,128)S(1)}, u32[]{:S(2)}, u32[]{:S(2)}) collective-permute-start(f32[16,256]{1,0:T(8,128)S(1)} %get-tuple-element.322), channel_id=1, source_target_pairs={{0,1},{1,2},{2,3},{3,4},{4,5},{5,6},{6,7},{7,8},{8,9},{9,10},{10,1... | collective-permute-start | bytes 49160 | tf_op jit(solution)/shard_map/while/body/eval_jaxpr/ppermute | solution.py:28
  486.8 7.7 %collective-permute-start.2 = (f32[16,256]{1,0:T(8,128)S(1)}, f32[16,256]{1,0:T(8,128)S(1)}, u32[]{:S(2)}, u32[]{:S(2)}) collective-permute-start(f32[16,256]{1,0:T(8,128)S(1)} %get-tuple-element.322), channel_id=1, source_target_pairs={{0,1},{1,2},{2,3},{3,4},{4,5},{5,6},{6,7},{7,8},{8,9},{9,10},{10,1... | collective-permute-start | bytes 49160 | tf_op jit(solution)/shard_map/while/body/eval_jaxpr/ppermute | solution.py:28
  495.2 7.7 %collective-permute-start.2 = (f32[16,256]{1,0:T(8,128)S(1)}, f32[16,256]{1,0:T(8,128)S(1)}, u32[]{:S(2)}, u32[]{:S(2)}) collective-permute-start(f32[16,256]{1,0:T(8,128)S(1)} %get-tuple-element.322), channel_id=1, source_target_pairs={{0,1},{1,2},{2,3},{3,4},{4,5},{5,6},{6,7},{7,8},{8,9},{9,10},{10,1... | collective-permute-start | bytes 49160 | tf_op jit(solution)/shard_map/while/body/eval_jaxpr/ppermute | solution.py:28
  503.5 7.7 %collective-permute-start.2 = (f32[16,256]{1,0:T(8,128)S(1)}, f32[16,256]{1,0:T(8,128)S(1)}, u32[]{:S(2)}, u32[]{:S(2)}) collective-permute-start(f32[16,256]{1,0:T(8,128)S(1)} %get-tuple-element.322), channel_id=1, source_target_pairs={{0,1},{1,2},{2,3},{3,4},{4,5},{5,6},{6,7},{7,8},{8,9},{9,10},{10,1... | collective-permute-start | bytes 49160 | tf_op jit(solution)/shard_map/while/body/eval_jaxpr/ppermute | solution.py:28
  511.8 7.7 %collective-permute-start.2 = (f32[16,256]{1,0:T(8,128)S(1)}, f32[16,256]{1,0:T(8,128)S(1)}, u32[]{:S(2)}, u32[]{:S(2)}) collective-permute-start(f32[16,256]{1,0:T(8,128)S(1)} %get-tuple-element.322), channel_id=1, source_target_pairs={{0,1},{1,2},{2,3},{3,4},{4,5},{5,6},{6,7},{7,8},{8,9},{9,10},{10,1... | collective-permute-start | bytes 49160 | tf_op jit(solution)/shard_map/while/body/eval_jaxpr/ppermute | solution.py:28
  520.2 7.7 %collective-permute-start.2 = (f32[16,256]{1,0:T(8,128)S(1)}, f32[16,256]{1,0:T(8,128)S(1)}, u32[]{:S(2)}, u32[]{:S(2)}) collective-permute-start(f32[16,256]{1,0:T(8,128)S(1)} %get-tuple-element.322), channel_id=1, source_target_pairs={{0,1},{1,2},{2,3},{3,4},{4,5},{5,6},{6,7},{7,8},{8,9},{9,10},{10,1... | collective-permute-start | bytes 49160 | tf_op jit(solution)/shard_map/while/body/eval_jaxpr/ppermute | solution.py:28
  528.5 7.9 %collective-permute-start.2 = (f32[16,256]{1,0:T(8,128)S(1)}, f32[16,256]{1,0:T(8,128)S(1)}, u32[]{:S(2)}, u32[]{:S(2)}) collective-permute-start(f32[16,256]{1,0:T(8,128)S(1)} %get-tuple-element.322), channel_id=1, source_target_pairs={{0,1},{1,2},{2,3},{3,4},{4,5},{5,6},{6,7},{7,8},{8,9},{9,10},{10,1... | collective-permute-start | bytes 49160 | tf_op jit(solution)/shard_map/while/body/eval_jaxpr/ppermute | solution.py:28
  537.0 7.7 %collective-permute-start.2 = (f32[16,256]{1,0:T(8,128)S(1)}, f32[16,256]{1,0:T(8,128)S(1)}, u32[]{:S(2)}, u32[]{:S(2)}) collective-permute-start(f32[16,256]{1,0:T(8,128)S(1)} %get-tuple-element.322), channel_id=1, source_target_pairs={{0,1},{1,2},{2,3},{3,4},{4,5},{5,6},{6,7},{7,8},{8,9},{9,10},{10,1... | collective-permute-start | bytes 49160 | tf_op jit(solution)/shard_map/while/body/eval_jaxpr/ppermute | solution.py:28
  545.3 7.7 %collective-permute-start.2 = (f32[16,256]{1,0:T(8,128)S(1)}, f32[16,256]{1,0:T(8,128)S(1)}, u32[]{:S(2)}, u32[]{:S(2)}) collective-permute-start(f32[16,256]{1,0:T(8,128)S(1)} %get-tuple-element.322), channel_id=1, source_target_pairs={{0,1},{1,2},{2,3},{3,4},{4,5},{5,6},{6,7},{7,8},{8,9},{9,10},{10,1... | collective-permute-start | bytes 49160 | tf_op jit(solution)/shard_map/while/body/eval_jaxpr/ppermute | solution.py:28
  553.7 7.7 %collective-permute-start.2 = (f32[16,256]{1,0:T(8,128)S(1)}, f32[16,256]{1,0:T(8,128)S(1)}, u32[]{:S(2)}, u32[]{:S(2)}) collective-permute-start(f32[16,256]{1,0:T(8,128)S(1)} %get-tuple-element.322), channel_id=1, source_target_pairs={{0,1},{1,2},{2,3},{3,4},{4,5},{5,6},{6,7},{7,8},{8,9},{9,10},{10,1... | collective-permute-start | bytes 49160 | tf_op jit(solution)/shard_map/while/body/eval_jaxpr/ppermute | solution.py:28
  562.0 7.7 %collective-permute-start.2 = (f32[16,256]{1,0:T(8,128)S(1)}, f32[16,256]{1,0:T(8,128)S(1)}, u32[]{:S(2)}, u32[]{:S(2)}) collective-permute-start(f32[16,256]{1,0:T(8,128)S(1)} %get-tuple-element.322), channel_id=1, source_target_pairs={{0,1},{1,2},{2,3},{3,4},{4,5},{5,6},{6,7},{7,8},{8,9},{9,10},{10,1... | collective-permute-start | bytes 49160 | tf_op jit(solution)/shard_map/while/body/eval_jaxpr/ppermute | solution.py:28
  572.2 8.0 %collective-permute-start.3 = (f32[16,256]{1,0:T(8,128)S(1)}, f32[16,256]{1,0:T(8,128)S(1)}, u32[]{:S(2)}, u32[]{:S(2)}) collective-permute-start(f32[16,256]{1,0:T(8,128)S(1)} %get-tuple-element.340), channel_id=1, source_target_pairs={{1,0},{2,1},{3,2},{4,3},{5,4},{6,5},{7,6},{8,7},{9,8},{10,9},{11,1... | collective-permute-start | bytes 49160 | tf_op jit(solution)/shard_map/while/body/eval_jaxpr/ppermute | solution.py:28
  580.8 7.7 %collective-permute-start.3 = (f32[16,256]{1,0:T(8,128)S(1)}, f32[16,256]{1,0:T(8,128)S(1)}, u32[]{:S(2)}, u32[]{:S(2)}) collective-permute-start(f32[16,256]{1,0:T(8,128)S(1)} %get-tuple-element.340), channel_id=1, source_target_pairs={{1,0},{2,1},{3,2},{4,3},{5,4},{6,5},{7,6},{8,7},{9,8},{10,9},{11,1... | collective-permute-start | bytes 49160 | tf_op jit(solution)/shard_map/while/body/eval_jaxpr/ppermute | solution.py:28
  589.1 7.7 %collective-permute-start.3 = (f32[16,256]{1,0:T(8,128)S(1)}, f32[16,256]{1,0:T(8,128)S(1)}, u32[]{:S(2)}, u32[]{:S(2)}) collective-permute-start(f32[16,256]{1,0:T(8,128)S(1)} %get-tuple-element.340), channel_id=1, source_target_pairs={{1,0},{2,1},{3,2},{4,3},{5,4},{6,5},{7,6},{8,7},{9,8},{10,9},{11,1... | collective-permute-start | bytes 49160 | tf_op jit(solution)/shard_map/while/body/eval_jaxpr/ppermute | solution.py:28
  597.4 7.7 %collective-permute-start.3 = (f32[16,256]{1,0:T(8,128)S(1)}, f32[16,256]{1,0:T(8,128)S(1)}, u32[]{:S(2)}, u32[]{:S(2)}) collective-permute-start(f32[16,256]{1,0:T(8,128)S(1)} %get-tuple-element.340), channel_id=1, source_target_pairs={{1,0},{2,1},{3,2},{4,3},{5,4},{6,5},{7,6},{8,7},{9,8},{10,9},{11,1... | collective-permute-start | bytes 49160 | tf_op jit(solution)/shard_map/while/body/eval_jaxpr/ppermute | solution.py:28
  605.8 7.7 %collective-permute-start.3 = (f32[16,256]{1,0:T(8,128)S(1)}, f32[16,256]{1,0:T(8,128)S(1)}, u32[]{:S(2)}, u32[]{:S(2)}) collective-permute-start(f32[16,256]{1,0:T(8,128)S(1)} %get-tuple-element.340), channel_id=1, source_target_pairs={{1,0},{2,1},{3,2},{4,3},{5,4},{6,5},{7,6},{8,7},{9,8},{10,9},{11,1... | collective-permute-start | bytes 49160 | tf_op jit(solution)/shard_map/while/body/eval_jaxpr/ppermute | solution.py:28
  614.1 7.7 %collective-permute-start.3 = (f32[16,256]{1,0:T(8,128)S(1)}, f32[16,256]{1,0:T(8,128)S(1)}, u32[]{:S(2)}, u32[]{:S(2)}) collective-permute-start(f32[16,256]{1,0:T(8,128)S(1)} %get-tuple-element.340), channel_id=1, source_target_pairs={{1,0},{2,1},{3,2},{4,3},{5,4},{6,5},{7,6},{8,7},{9,8},{10,9},{11,1... | collective-permute-start | bytes 49160 | tf_op jit(solution)/shard_map/while/body/eval_jaxpr/ppermute | solution.py:28
  622.5 7.7 %collective-permute-start.3 = (f32[16,256]{1,0:T(8,128)S(1)}, f32[16,256]{1,0:T(8,128)S(1)}, u32[]{:S(2)}, u32[]{:S(2)}) collective-permute-start(f32[16,256]{1,0:T(8,128)S(1)} %get-tuple-element.340), channel_id=1, source_target_pairs={{1,0},{2,1},{3,2},{4,3},{5,4},{6,5},{7,6},{8,7},{9,8},{10,9},{11,1... | collective-permute-start | bytes 49160 | tf_op jit(solution)/shard_map/while/body/eval_jaxpr/ppermute | solution.py:28
  630.8 7.9 %collective-permute-start.3 = (f32[16,256]{1,0:T(8,128)S(1)}, f32[16,256]{1,0:T(8,128)S(1)}, u32[]{:S(2)}, u32[]{:S(2)}) collective-permute-start(f32[16,256]{1,0:T(8,128)S(1)} %get-tuple-element.340), channel_id=1, source_target_pairs={{1,0},{2,1},{3,2},{4,3},{5,4},{6,5},{7,6},{8,7},{9,8},{10,9},{11,1... | collective-permute-start | bytes 49160 | tf_op jit(solution)/shard_map/while/body/eval_jaxpr/ppermute | solution.py:28
  639.3 7.7 %collective-permute-start.3 = (f32[16,256]{1,0:T(8,128)S(1)}, f32[16,256]{1,0:T(8,128)S(1)}, u32[]{:S(2)}, u32[]{:S(2)}) collective-permute-start(f32[16,256]{1,0:T(8,128)S(1)} %get-tuple-element.340), channel_id=1, source_target_pairs={{1,0},{2,1},{3,2},{4,3},{5,4},{6,5},{7,6},{8,7},{9,8},{10,9},{11,1... | collective-permute-start | bytes 49160 | tf_op jit(solution)/shard_map/while/body/eval_jaxpr/ppermute | solution.py:28
  (173 other events, 2091.0 us)
where the time goes:
time: 704 us; the launch traced here: 701 us
  starting transfers between devices  336 us (48%)
  waiting for transfers between devices  292 us (41%)
  local copies, waits for them, and re-layouts  44.5 us (6%)
  matrix products  22.2 us (3%)
    ppermute x92, starting transfers between devices, passed_along(): return lax.ppermute(x, axis, pairs)  323 us
    ppermute x92, waiting for transfers between devices, passed_along(): return lax.ppermute(x, axis, pairs)  290 us
    while x184, local copies, waits for them, and re-layouts  36.8 us
    dot_general x98, matrix products, apply_map(): jnp.dot(state, matrix, precision=HIGHEST_MODE, preferred_element_type=jnp...  22.2 us
  transfers between devices with their start and end apart: 96, of which 93 were waited for; matrix products, arithmetic and copies ran while one was open for 0% of the time, Pallas kernels for 0%

commit v1 on v0

v1 whole, which is shorter than its diff:
```python
import functools

import jax
import jax.numpy as jnp
from jax import lax
from jax.experimental import pallas as pl
from jax.experimental.pallas import tpu as pltpu
from jax.sharding import PartitionSpec as P

Z = 16
E = 16
C = 16
K = 256
NX_DEV = 32
NY_DEV = 16
G = 4
MESH = pl.DeviceIdType.MESH

HALO = 0
FX, BX, FY, BY = 4, 7, 10, 13
SX, QX, SY, QY = 16, 19, 22, 25
EXF, EXB, EYF, EYB = 28, 29, 30, 31
COPIES = 32


def split(x):
    high = x.astype(jnp.bfloat16)
    low = (x - high.astype(jnp.float32)).astype(jnp.bfloat16)
    return high, low


def product(state, wide):
    high, low = split(state)
    r = jnp.dot(
        jnp.concatenate([high, low], axis=0), wide, preferred_element_type=jnp.float32
    )
    return (r[E:, K:] + r[:E, K:] + r[E:, :K]) + r[:E, :K]


def kernel(
    start_ref, classes_ref, conductor_ref, drive_ref, perm_ref, leaf_x_ref, leaf_y_ref,
    fwd_x_ref, back_x_ref, couple_x_ref, fwd_y_ref, back_y_ref, couple_y_ref,
    out_ref,
    edge_out, edge_in, row_in, resid_ref, permit_ref,
    got_x, got_y, wide_x, wide_y, wide_c,
    src_ref, state_out, state_in, across_ref, along_ref,
    send_sem, recv_sem,
):
    i = lax.axis_index("gx")
    j = lax.axis_index("gy")
    ix, gx = i % G, i // G
    jy, gy = j % G, j // G
    core, chip = ix % 2, ix // 2

    def at_x(index):
        return (index, j)

    def at_y(index):
        return (i, index)

    xp = [
        gx * G + 2 * chip + (1 - core),
        gx * G + 2 * (1 - chip) + core,
        gx * G + 2 * (1 - chip) + (1 - core),
    ]
    yp = [gy * G + (jy + d) % G for d in (1, 2, 3)]

    def slot_x(k):
        return 2 * ((chip + k // 2) % 2) + (core + k % 2) % 2

    def slot_y(k):
        return (jy + G - k) % G

    partners = [(None, at_x(p)) for p in xp] + [(None, at_y(p)) for p in yp]
    partners += [
        ((ix == 0) & (i > 0), at_x(i - 1)),
        ((ix == G - 1) & (i < NX_DEV - 1), at_x(i + 1)),
        (i >= G, at_x(i - G)),
        (i < NX_DEV - G, at_x(i + G)),
        ((jy == 0) & (j > 0), at_y(j - 1)),
        ((jy == G - 1) & (j < NY_DEV - 1), at_y(j + 1)),
        (j >= G, at_y(j - G)),
        (j < NY_DEV - G, at_y(j + G)),
    ]
    barrier = pltpu.get_barrier_semaphore()
    for held, where in partners:
        def greet(where=where):
            pl.semaphore_signal(barrier, inc=1, device_id=where, device_id_type=MESH)
        if held is None:
            greet()
        else:
            pl.when(held)(greet)
    edge_out[0] = start_ref[:, C - 1, :]
    edge_out[1] = start_ref[:, 0, :]
    count = 6
    for held, _ in partners[6:]:
        count = count + held.astype(jnp.int32)
    pl.semaphore_wait(barrier, count)

    def copy(src, dst, number, where):
        return pltpu.make_async_remote_copy(
            src_ref=src, dst_ref=dst, send_sem=send_sem.at[number],
            recv_sem=recv_sem.at[number], device_id=where, device_id_type=MESH,
        )

    halo = [
        (i < NX_DEV - 1, i > 0, copy(edge_out.at[0], edge_in.at[0], HALO, at_x(i + 1))),
        (i > 0, i < NX_DEV - 1, copy(edge_out.at[1], edge_in.at[1], HALO + 1, at_x(i - 1))),
        (j < NY_DEV - 1, j > 0,
         copy(start_ref.at[:, :, pl.ds(K // 2, K // 2)], row_in.at[0], HALO + 2, at_y(j + 1))),
        (j > 0, j < NY_DEV - 1,
         copy(start_ref.at[:, :, pl.ds(0, K // 2)], row_in.at[1], HALO + 3, at_y(j - 1))),
    ]
    for sends, _, move in halo:
        pl.when(sends)(move.start)

    ops_x = []
    for n, (ref, number) in enumerate(((fwd_x_ref, FX), (back_x_ref, BX))):
        ops_x.append([
            copy(ref, got_x.at[n, 0], number, at_x(xp[0])),
            copy(ref, got_x.at[n, 1], number + 1, at_x(xp[1])),
            copy(got_x.at[n, 1], got_x.at[n, 2], number + 2, at_x(xp[0])),
        ])
    ops_y = []
    for n, (ref, number) in enumerate(((fwd_y_ref, FY), (back_y_ref, BY))):
        ops_y.append([
            copy(ref, got_y.at[n, d], number + d, at_y(yp[d])) for d in range(3)
        ])
    for n in range(2):
        ops_x[n][1].start()
        ops_x[n][0].start()
    for n in range(2):
        for move in ops_y[n]:
            move.start()

    def widen(ref, target):
        high, low = split(ref[...])
        target[:, :K] = high
        target[:, K:] = low

    widen(couple_x_ref, wide_c.at[0])
    widen(couple_y_ref, wide_c.at[1])
    widen(fwd_x_ref, wide_x.at[0, 0])
    widen(back_x_ref, wide_x.at[1, 0])
    widen(fwd_y_ref, wide_y.at[0, 0])
    widen(back_y_ref, wide_y.at[1, 0])

    permit = jnp.zeros((C, K), jnp.float32)
    for c in range(8):
        permit = jnp.where(classes_ref[...] == c, perm_ref[c], permit)
    permit_ref[...] = permit

    lane = lax.broadcasted_iota(jnp.int32, (C, K), 1)
    col = lax.broadcasted_iota(jnp.int32, (C, K), 0)
    node = lane % Z
    mine = lane // Z == col

    for n, target in ((0, edge_in.at[0]), (1, edge_in.at[1]), (2, row_in.at[0]), (3, row_in.at[1])):
        _, receives, move = halo[n]
        pl.when(receives)(move.wait_recv)

        def clear(target=target):
            target[...] = jnp.zeros(target.shape, jnp.float32)
        pl.when(jnp.logical_not(receives))(clear)

    def residual(e, _):
        x = start_ref[e]
        low = edge_in[0, pl.ds(e, 1), :]
        high = edge_in[1, pl.ds(e, 1), :]
        after = jnp.where(col == C - 1, high, pltpu.roll(x, C - 1, 0))
        before = jnp.where(col == 0, low, pltpu.roll(x, 1, 0))
        piece = row_in[0, e]
        row_before = pltpu.roll(
            jnp.where(lane >= K - Z, jnp.concatenate([piece, piece], axis=1), x), Z, 1)
        piece = row_in[1, e]
        row_after = pltpu.roll(
            jnp.where(lane < Z, jnp.concatenate([piece, piece], axis=1), x), K - Z, 1)
        beside = after + before + row_after + row_before
        upper = jnp.where(node == Z - 1, 0.0, pltpu.roll(x, K - 1, 1))
        lower = jnp.where(node == 0, 0.0, pltpu.roll(x, 1, 1))
        source = jnp.where(conductor_ref[...] == e, drive_ref[...], 0.0)
        resid = source - (permit_ref[...] * (4.0 * x - beside) + 2.0 * x - (upper + lower))
        resid_ref[e] = resid
        src_ref[0, 0, pl.ds(e, 1), :] = jnp.sum(leaf_x_ref[...] * resid, axis=0, keepdims=True)
        return 0

    lax.fori_loop(0, E, residual, 0)

    def share(n, number, places):
        moves = [
            copy(src_ref.at[n, 0], src_ref.at[n, d + 1], number + d, places[d])
            for d in range(3)
        ]
        for move in reversed(moves):
            move.start()
        return moves

    def sweep(n, moves, wide, way, slot, order, position, first, last, number, to):
        for move in moves:
            move.wait_recv()
        step = copy(state_out.at[n], state_in.at[n], number, to)

        def clear():
            state_in[n] = jnp.zeros((E, K), jnp.float32)
        pl.when(first)(clear)
        pl.when(jnp.logical_not(first))(step.wait_recv)
        state = state_in[n]
        kept = jnp.zeros((E, K), jnp.float32)
        for k in order:
            s = slot(k)
            state = product(state, wide[way, s]) + src_ref[n, s]
            kept = jnp.where(position == k, state, kept)
        state_out[n] = state
        pl.when(jnp.logical_not(last))(step.start)
        return kept, step

    up, down = (0, 1, 2, 3), (3, 2, 1, 0)
    x_first, x_last = i < G, i >= NX_DEV - G
    y_first, y_last = j < G, j >= NY_DEV - G
    to_xf = at_x(i + G)
    to_xb = at_x(i - G)

    moves_sx = share(0, SX, [at_x(p) for p in xp])
    for n in range(2):
        ops_x[n][1].wait_recv()
        ops_x[n][2].start()
        widen(got_x.at[n, 1], wide_x.at[n, 2])
        ops_x[n][0].wait_recv()
        widen(got_x.at[n, 0], wide_x.at[n, 1])
        if n == 0:
            ops_x[n][2].wait_recv()
            widen(got_x.at[n, 2], wide_x.at[n, 3])
            ahead, step_xf = sweep(
                0, moves_sx, wide_x, 0, slot_x, up, ix, x_first, x_last, EXF, to_xf)
            src_ref[1, 0] = product(ahead, wide_c[0])
            moves_qx = share(1, QX, [at_x(p) for p in xp])
    ops_x[1][2].wait_recv()
    widen(got_x.at[1, 2], wide_x.at[1, 3])
    across, step_xb = sweep(
        1, moves_qx, wide_x, 1, slot_x, down, ix, x_last, x_first, EXB, to_xb)
    across_ref[...] = across

    def gather_y(e, _):
        lifted = resid_ref[e] + leaf_x_ref[...] * across_ref[pl.ds(e, 1), :]
        t = lifted * leaf_y_ref[...]
        for shift in (128, 64, 32, 16):
            t = t + pltpu.roll(t, shift, 1)
        src_ref[2, 0, pl.ds(e, 1), :] = jnp.sum(jnp.where(mine, t, 0.0), axis=0, keepdims=True)
        return 0

    lax.fori_loop(0, E, gather_y, 0)
    moves_sy = share(2, SY, [at_y(p) for p in yp])
    for n in range(2):
        for d in range(3):
            ops_y[n][d].wait_recv()
            widen(got_y.at[n, d], wide_y.at[n, d + 1])
    ahead, step_yf = sweep(
        2, moves_sy, wide_y, 0, slot_y, up, jy, y_first, y_last, EYF, at_y(j + G))
    src_ref[3, 0] = product(ahead, wide_c[1])
    moves_qy = share(3, QY, [at_y(p) for p in yp])
    along, step_yb = sweep(
        3, moves_qy, wide_y, 1, slot_y, down, jy, y_last, y_first, EYB, at_y(j - G))
    along_ref[...] = along

    def finish(e, _):
        t = jnp.where(mine, along_ref[pl.ds(e, 1), :], 0.0)
        for shift in (128, 64, 32, 16):
            t = t + pltpu.roll(t, shift, 1)
        out_ref[e] = (
            start_ref[e] + leaf_x_ref[...] * across_ref[pl.ds(e, 1), :] + leaf_y_ref[...] * t
        )
        return 0

    lax.fori_loop(0, E, finish, 0)

    for sends, _, move in halo:
        pl.when(sends)(move.wait_send)
    for moves in ops_x + ops_y + [moves_sx, moves_qx, moves_sy, moves_qy]:
        for move in moves:
            move.wait_send()
    pl.when(jnp.logical_not(x_last))(step_xf.wait_send)
    pl.when(jnp.logical_not(x_first))(step_xb.wait_send)
    pl.when(jnp.logical_not(y_last))(step_yf.wait_send)
    pl.when(jnp.logical_not(y_first))(step_yb.wait_send)


def local(*arrays):
    vmem = pl.BlockSpec(memory_space=pltpu.VMEM)
    smem = pl.BlockSpec(memory_space=pltpu.SMEM)
    f32, bf16 = jnp.float32, jnp.bfloat16
    return pl.pallas_call(
        kernel,
        out_shape=jax.ShapeDtypeStruct((E, C, K), f32),
        in_specs=[vmem] * 4 + [smem] + [vmem] * 8,
        out_specs=vmem,
        scratch_shapes=[
            pltpu.VMEM((2, E, K), f32),
            pltpu.VMEM((2, E, K), f32),
            pltpu.VMEM((2, E, C, K // 2), f32),
            pltpu.VMEM((E, C, K), f32),
            pltpu.VMEM((C, K), f32),
            pltpu.VMEM((2, 3, K, K), f32),
            pltpu.VMEM((2, 3, K, K), f32),
            pltpu.VMEM((2, G, K, 2 * K), bf16),
            pltpu.VMEM((2, G, K, 2 * K), bf16),
            pltpu.VMEM((2, K, 2 * K), bf16),
            pltpu.VMEM((4, G, E, K), f32),
            pltpu.VMEM((4, E, K), f32),
            pltpu.VMEM((4, E, K), f32),
            pltpu.VMEM((E, K), f32),
            pltpu.VMEM((E, K), f32),
            pltpu.SemaphoreType.DMA((COPIES,)),
            pltpu.SemaphoreType.DMA((COPIES,)),
        ],
        compiler_params=pltpu.CompilerParams(
            collective_id=0, has_side_effects=True, vmem_limit_bytes=48 * 1024 * 1024
        ),
    )(*arrays)


def solution(mesh):
    split_two = P("gx", "gy")
    in_specs = (P(None, "gx", "gy"),) + (split_two,) * 3 + (P(),) + (split_two,) * 8
    return jax.shard_map(
        local, mesh=mesh, in_specs=in_specs, out_specs=P(None, "gx", "gy"), check_vma=False
    )
```

time: 704 us -> 133 us (0.19)
  the two profiles are of different devices: /device:TPU:406 before, /device:TPU:6 now
where the time goes in v1:
time: 133 us
  Pallas kernels  121 us (91%)
  local copies, waits for them, and re-layouts  11.6 us (9%)
    pallas_call x1, Pallas kernels, local(): pl.pallas_call(kernel, out_shape=jax.ShapeDtypeStruct((E, C, K), f32), in...  121 us
    unnamed x27, local copies, waits for them, and re-layouts  11.6 us

profile of v1, /device:TPU:6, one launch (start us, length us, event | category | flops | bytes accessed | tf_op | source)
XLA Modules:
  0.0 132.9 jit_solution(5508898548677032261)
XLA Ops:
  0.0 0.0 copy-start
  0.0 0.9 copy-done
  1.0 0.0 copy-start.1
  1.0 0.9 copy-done.1
  1.9 0.0 copy-start.2
  1.9 0.9 copy-done.2
  2.9 0.0 copy-start.3
  2.9 0.9 copy-done.3
  3.8 0.0 copy-start.4
  3.8 0.9 copy-done.4
  4.8 0.0 copy-start.5
  4.8 0.9 copy-done.5
  5.7 0.0 copy-start.6
  5.7 0.9 copy-done.6
  6.7 0.0 copy-start.7
  6.7 0.7 copy-done.7
  7.4 0.0 copy-start.8
  7.4 0.7 copy-done.8
  8.1 0.7 copy-done.9
  8.8 0.7 copy-done.10
  9.5 0.7 copy-done.11
  10.2 0.7 copy-done.12
  10.9 121.3 %shard_map.127 = f32[16,16,256]{2,1,0:T(8,128)S(1)} custom-call(f32[16,16,256]{2,1,0:T(8,128)S(1)} %copy-done, s32[16,256]{1,0:T(8,128)S(1)} %copy-done.7, s32[16,256]{1,0:T(8,128)S(1)} %copy-done.8, f32[16,256]{1,0:T(8,128)S(1)} %copy-done.9, f32[8]{0:T(128)S(1)} %copy-done.12, f32[16,256]{1,0:T(8,128)S(1)} %copy-done.10, f32[16,256]{1,0:T(8,128)S(1)} %copy-done.11, ...), custom_call_target="tpu_custom_call" | custom-call | tf_op jit(solution)/shard_map/pallas_call | solution.py:291
  132.2 0.7 copy.15
  (4 shorter events, 0.0 us)
Async XLA Ops:
  0.0 0.9 copy-start
  1.0 0.9 copy-start.1
  1.9 0.9 copy-start.2
  2.9 0.9 copy-start.3
  3.8 0.9 copy-start.4
  4.8 0.9 copy-start.5
  5.7 0.9 copy-start.6
  6.7 0.7 copy-start.7
  7.4 0.7 copy-start.8
  8.1 0.7 copy-start.9
  8.8 0.7 copy-start.10
  9.5 0.7 copy-start.11
  10.2 0.7 copy-start.12

commit v2 on v1

--- a/solution.py
+++ b/solution.py
@@ -22,6 +22,9 @@
 EXF, EXB, EYF, EYB = 28, 29, 30, 31
 COPIES = 32
 
+DOWN, UP = 2.0**-24, 2.0**24
+ROWS = 128
+
 
 def split(x):
     high = x.astype(jnp.bfloat16)
@@ -29,12 +32,16 @@
     return high, low
 
 
-def product(state, wide):
-    high, low = split(state)
+def product_of(high, low, wide):
+    rows = high.shape[0]
     r = jnp.dot(
         jnp.concatenate([high, low], axis=0), wide, preferred_element_type=jnp.float32
     )
-    return (r[E:, K:] + r[:E, K:] + r[E:, :K]) + r[:E, :K]
+    return (r[rows:, K:] + r[:rows, K:] + r[rows:, :K]) + r[:rows, :K]
+
+
+def product(state, wide):
+    return product_of(*split(state), wide)
 
 
 def kernel(
@@ -42,8 +49,8 @@
     fwd_x_ref, back_x_ref, couple_x_ref, fwd_y_ref, back_y_ref, couple_y_ref,
     out_ref,
     edge_out, edge_in, row_in, resid_ref, permit_ref,
-    got_x, got_y, wide_x, wide_y, wide_c,
-    src_ref, state_out, state_in, across_ref, along_ref,
+    got_x, got_y, wide_x, wide_y, wide_c, whole_ref, prefix_ref,
+    src_ref, kept_ref, tail_ref, state_out, state_in, across_ref, along_ref,
     send_sem, recv_sem,
 ):
     i = lax.axis_index("gx")
@@ -195,50 +202,102 @@
             move.start()
         return moves
 
-    def sweep(n, moves, wide, way, slot, order, position, first, last, number, to):
+    def compose(n, wide, way, slot, order, position):
+        def part(h, _):
+            rows = pl.ds(pl.multiple_of(h * ROWS, ROWS), ROWS)
+
+            def put(target, x):
+                high, low = split(x * DOWN)
+                target[n, rows, :K] = high
+                target[n, rows, K:] = low
+
+            pair = wide[way, slot(order[0]), rows, :]
+            high, low = pair[:, :K], pair[:, K:]
+            x = high.astype(jnp.float32) + low.astype(jnp.float32)
+            pl.when(position == order[0])(functools.partial(put, prefix_ref, x))
+            for k in order[1:]:
+                x = product_of(high, low, wide[way, slot(k)])
+                pl.when(position == k)(functools.partial(put, prefix_ref, x))
+                high, low = split(x)
+            put(whole_ref, x)
+            return 0
+
+        lax.fori_loop(0, K // ROWS, part, 0)
+
+    def step_of(n, number, to):
+        return copy(state_out.at[n], state_in.at[n], number, to)
+
+    def inside(n, moves, wide, way, slot, order, position, first, step):
         for move in moves:
             move.wait_recv()
-        step = copy(state_out.at[n], state_in.at[n], number, to)
-
-        def clear():
+        state = src_ref[n, slot(order[0])] * DOWN
+        kept = state
+        for k in order[1:]:
+            s = slot(k)
+            state = product(state, wide[way, s]) + src_ref[n, s] * DOWN
+            kept = jnp.where(position == k, state, kept)
+        kept_ref[n] = kept
+        tail_ref[n] = state
+
+        def begin():
+            state_out[n] = state * UP
+            step.start()
             state_in[n] = jnp.zeros((E, K), jnp.float32)
-        pl.when(first)(clear)
-        pl.when(jnp.logical_not(first))(step.wait_recv)
-        state = state_in[n]
-        kept = jnp.zeros((E, K), jnp.float32)
-        for k in order:
-            s = slot(k)
-            state = product(state, wide[way, s]) + src_ref[n, s]
-            kept = jnp.where(position == k, state, kept)
-        state_out[n] = state
-        pl.when(jnp.logical_not(last))(step.start)
-        return kept, step
+        pl.when(first)(begin)
+
+    def across_groups(n, first, last, step):
+        def take():
+            step.wait_recv()
+        pl.when(jnp.logical_not(first))(take)
+
+        def give():
+            state_out[n] = (product(state_in[n], whole_ref[n]) + tail_ref[n]) * UP
+            step.start()
+        pl.when(jnp.logical_not(first) & jnp.logical_not(last))(give)
+        return (product(state_in[n], prefix_ref[n]) + kept_ref[n]) * UP
 
     up, down = (0, 1, 2, 3), (3, 2, 1, 0)
     x_first, x_last = i < G, i >= NX_DEV - G
     y_first, y_last = j < G, j >= NY_DEV - G
-    to_xf = at_x(i + G)
-    to_xb = at_x(i - G)
-
-    moves_sx = share(0, SX, [at_x(p) for p in xp])
-    for n in range(2):
+    step_xf = step_of(0, EXF, at_x(i + G))
+    step_xb = step_of(1, EXB, at_x(i - G))
+    step_yf = step_of(2, EYF, at_y(j + G))
+    step_yb = step_of(3, EYB, at_y(j - G))
+    early = i < NX_DEV // 2
+    late = jnp.logical_not(early)
+
+    def receive_x(n):
         ops_x[n][1].wait_recv()
         ops_x[n][2].start()
         widen(got_x.at[n, 1], wide_x.at[n, 2])
         ops_x[n][0].wait_recv()
         widen(got_x.at[n, 0], wide_x.at[n, 1])
-        if n == 0:
-            ops_x[n][2].wait_recv()
-            widen(got_x.at[n, 2], wide_x.at[n, 3])
-            ahead, step_xf = sweep(
-                0, moves_sx, wide_x, 0, slot_x, up, ix, x_first, x_last, EXF, to_xf)
-            src_ref[1, 0] = product(ahead, wide_c[0])
-            moves_qx = share(1, QX, [at_x(p) for p in xp])
-    ops_x[1][2].wait_recv()
-    widen(got_x.at[1, 2], wide_x.at[1, 3])
-    across, step_xb = sweep(
-        1, moves_qx, wide_x, 1, slot_x, down, ix, x_last, x_first, EXB, to_xb)
-    across_ref[...] = across
+        ops_x[n][2].wait_recv()
+        widen(got_x.at[n, 2], wide_x.at[n, 3])
+
+    def ready_back_x():
+        receive_x(1)
+        compose(1, wide_x, 1, slot_x, down, ix)
+
+    def ready_y():
+        for n, order in ((0, up), (1, down)):
+            for d in range(3):
+                ops_y[n][d].wait_recv()
+                widen(got_y.at[n, d], wide_y.at[n, d + 1])
+            compose(2 + n, wide_y, n, slot_y, order, jy)
+
+    moves_sx = share(0, SX, [at_x(p) for p in xp])
+    receive_x(0)
+    inside(0, moves_sx, wide_x, 0, slot_x, up, ix, x_first, step_xf)
+    compose(0, wide_x, 0, slot_x, up, ix)
+    pl.when(late)(ready_back_x)
+    ahead = across_groups(0, x_first, x_last, step_xf)
+    src_ref[1, 0] = product(ahead, wide_c[0])
+    moves_qx = share(1, QX, [at_x(p) for p in xp])
+    pl.when(early)(ready_back_x)
+    inside(1, moves_qx, wide_x, 1, slot_x, down, ix, x_last, step_xb)
+    pl.when(early)(ready_y)
+    across_ref[...] = across_groups(1, x_last, x_first, step_xb)
 
     def gather_y(e, _):
         lifted = resid_ref[e] + leaf_x_ref[...] * across_ref[pl.ds(e, 1), :]
@@ -250,17 +309,13 @@
 
     lax.fori_loop(0, E, gather_y, 0)
     moves_sy = share(2, SY, [at_y(p) for p in yp])
-    for n in range(2):
-        for d in range(3):
-            ops_y[n][d].wait_recv()
-            widen(got_y.at[n, d], wide_y.at[n, d + 1])
-    ahead, step_yf = sweep(
-        2, moves_sy, wide_y, 0, slot_y, up, jy, y_first, y_last, EYF, at_y(j + G))
+    pl.when(late)(ready_y)
+    inside(2, moves_sy, wide_y, 0, slot_y, up, jy, y_first, step_yf)
+    ahead = across_groups(2, y_first, y_last, step_yf)
     src_ref[3, 0] = product(ahead, wide_c[1])
     moves_qy = share(3, QY, [at_y(p) for p in yp])
-    along, step_yb = sweep(
-        3, moves_qy, wide_y, 1, slot_y, down, jy, y_last, y_first, EYB, at_y(j - G))
-    along_ref[...] = along
+    inside(3, moves_qy, wide_y, 1, slot_y, down, jy, y_last, step_yb)
+    along_ref[...] = across_groups(3, y_last, y_first, step_yb)
 
     def finish(e, _):
         t = jnp.where(mine, along_ref[pl.ds(e, 1), :], 0.0)
@@ -304,7 +359,11 @@
             pltpu.VMEM((2, G, K, 2 * K), bf16),
             pltpu.VMEM((2, G, K, 2 * K), bf16),
             pltpu.VMEM((2, K, 2 * K), bf16),
+            pltpu.VMEM((4, K, 2 * K), bf16),
+            pltpu.VMEM((4, K, 2 * K), bf16),
             pltpu.VMEM((4, G, E, K), f32),
+            pltpu.VMEM((4, E, K), f32),
+            pltpu.VMEM((4, E, K), f32),
             pltpu.VMEM((4, E, K), f32),
             pltpu.VMEM((4, E, K), f32),
             pltpu.VMEM((E, K), f32),

time: 133 us -> 123 us (0.925)
  Pallas kernels: 121 us -> 111 us
    pallas_call x1, Pallas kernels: 121 us -> 111 us  [local(): pl.pallas_call(kernel, out_shape=jax.ShapeDtypeStruct((E, C, K), f32), in...]
where the time goes in v2:
time: 123 us; the launch traced here: 122 us
  Pallas kernels  111 us (90%)
  local copies, waits for them, and re-layouts  11.6 us (9%)
    pallas_call x1, Pallas kernels, local(): pl.pallas_call(kernel, out_shape=jax.ShapeDtypeStruct((E, C, K), f32), in...  111 us
    unnamed x27, local copies, waits for them, and re-layouts  11.6 us

profile of v2, /device:TPU:6, one launch (start us, length us, event | category | flops | bytes accessed | tf_op | source)
XLA Modules:
  0.0 122.2 jit_solution(14997744766175066880)
XLA Ops:
  0.0 0.0 copy-start
  0.0 0.9 copy-done
  1.0 0.0 copy-start.1
  1.0 0.9 copy-done.1
  1.9 0.0 copy-start.2
  1.9 0.9 copy-done.2
  2.9 0.0 copy-start.3
  2.9 0.9 copy-done.3
  3.8 0.0 copy-start.4
  3.8 0.9 copy-done.4
  4.8 0.0 copy-start.5
  4.8 0.9 copy-done.5
  5.7 0.0 copy-start.6
  5.7 0.9 copy-done.6
  6.7 0.0 copy-start.7
  6.7 0.7 copy-done.7
  7.4 0.0 copy-start.8
  7.4 0.7 copy-done.8
  8.1 0.7 copy-done.9
  8.8 0.7 copy-done.10
  9.5 0.7 copy-done.11
  10.2 0.7 copy-done.12
  10.9 110.6 %shard_map.127 = f32[16,16,256]{2,1,0:T(8,128)S(1)} custom-call(f32[16,16,256]{2,1,0:T(8,128)S(1)} %copy-done, s32[16,256]{1,0:T(8,128)S(1)} %copy-done.7, s32[16,256]{1,0:T(8,128)S(1)} %copy-done.8, f32[16,256]{1,0:T(8,128)S(1)} %copy-done.9, f32[8]{0:T(128)S(1)} %copy-done.12, f32[16,256]{1,0:T(8,128)S(1)} %copy-done.10, f32[16,256]{1,0:T(8,128)S(1)} %copy-done.11, ...), custom_call_target="tpu_custom_call" | custom-call | tf_op jit(solution)/shard_map/pallas_call | solution.py:346
  121.5 0.7 copy.15
  (4 shorter events, 0.0 us)
Async XLA Ops:
  0.0 0.9 copy-start
  1.0 0.9 copy-start.1
  1.9 0.9 copy-start.2
  2.9 0.9 copy-start.3
  3.8 0.9 copy-start.4
  4.8 0.9 copy-start.5
  5.7 0.9 copy-start.6
  6.7 0.7 copy-start.7
  7.4 0.7 copy-start.8
  8.1 0.7 copy-start.9
  8.8 0.7 copy-start.10
  9.5 0.7 copy-start.11
  10.2 0.7 copy-start.12

commit v3 on v2

--- a/solution.py
+++ b/solution.py
@@ -19,8 +19,12 @@
 HALO = 0
 FX, BX, FY, BY = 4, 7, 10, 13
 SX, QX, SY, QY = 16, 19, 22, 25
-EXF, EXB, EYF, EYB = 28, 29, 30, 31
-COPIES = 32
+EXF, EXB = 28, 29
+WY = 30
+TY = 36
+COPIES = 48
+WHOLE_PAIRS = ((1, 2), (1, 3), (2, 3))
+TAIL_PAIRS = ((0, 1), (0, 2), (0, 3), (1, 2), (1, 3), (2, 3))
 
 DOWN, UP = 2.0**-24, 2.0**24
 ROWS = 128
@@ -49,8 +53,8 @@
     fwd_x_ref, back_x_ref, couple_x_ref, fwd_y_ref, back_y_ref, couple_y_ref,
     out_ref,
     edge_out, edge_in, row_in, resid_ref, permit_ref,
-    got_x, got_y, wide_x, wide_y, wide_c, whole_ref, prefix_ref,
-    src_ref, kept_ref, tail_ref, state_out, state_in, across_ref, along_ref,
+    got_x, got_y, wide_x, wide_y, wide_c, whole_ref, prefix_ref, whole_out, whole_in, wide_in,
+    src_ref, kept_ref, tail_ref, state_out, state_in, tails_in, across_ref, along_ref,
     send_sem, recv_sem,
 ):
     i = lax.axis_index("gx")
@@ -79,6 +83,7 @@
         return (jy + G - k) % G
 
     partners = [(None, at_x(p)) for p in xp] + [(None, at_y(p)) for p in yp]
+    partners += [(None, at_y((gy + q) % G * G + jy)) for q in (1, 2, 3)]
     partners += [
         ((ix == 0) & (i > 0), at_x(i - 1)),
         ((ix == G - 1) & (i < NX_DEV - 1), at_x(i + 1)),
@@ -86,8 +91,6 @@
         (i < NX_DEV - G, at_x(i + G)),
         ((jy == 0) & (j > 0), at_y(j - 1)),
         ((jy == G - 1) & (j < NY_DEV - 1), at_y(j + 1)),
-        (j >= G, at_y(j - G)),
-        (j < NY_DEV - G, at_y(j + G)),
     ]
     barrier = pltpu.get_barrier_semaphore()
     for held, where in partners:
@@ -99,8 +102,8 @@
             pl.when(held)(greet)
     edge_out[0] = start_ref[:, C - 1, :]
     edge_out[1] = start_ref[:, 0, :]
-    count = 6
-    for held, _ in partners[6:]:
+    count = 9
+    for held, _ in partners[9:]:
         count = count + held.astype(jnp.int32)
     pl.semaphore_wait(barrier, count)
 
@@ -133,12 +136,8 @@
         ops_y.append([
             copy(ref, got_y.at[n, d], number + d, at_y(yp[d])) for d in range(3)
         ])
-    for n in range(2):
-        ops_x[n][1].start()
-        ops_x[n][0].start()
-    for n in range(2):
-        for move in ops_y[n]:
-            move.start()
+    ops_x[0][1].start()
+    ops_x[0][0].start()
 
     def widen(ref, target):
         high, low = split(ref[...])
@@ -220,6 +219,8 @@
                 pl.when(position == k)(functools.partial(put, prefix_ref, x))
                 high, low = split(x)
             put(whole_ref, x)
+            if n >= 2:
+                whole_out[n - 2, rows, :] = x * DOWN
             return 0
 
         lax.fori_loop(0, K // ROWS, part, 0)
@@ -227,7 +228,7 @@
     def step_of(n, number, to):
         return copy(state_out.at[n], state_in.at[n], number, to)
 
-    def inside(n, moves, wide, way, slot, order, position, first, step):
+    def inside(n, moves, wide, way, slot, order, position, first=None, step=None):
         for move in moves:
             move.wait_recv()
         state = src_ref[n, slot(order[0])] * DOWN
@@ -237,6 +238,11 @@
             state = product(state, wide[way, s]) + src_ref[n, s] * DOWN
             kept = jnp.where(position == k, state, kept)
         kept_ref[n] = kept
+        if step is None:
+            state_out[n] = state
+            for a, _, move in tails[n - 2]:
+                pl.when(rank[n - 2] == a)(move.start)
+            return
         tail_ref[n] = state
 
         def begin():
@@ -256,15 +262,42 @@
         pl.when(jnp.logical_not(first) & jnp.logical_not(last))(give)
         return (product(state_in[n], prefix_ref[n]) + kept_ref[n]) * UP
 
+    def entry_y(n):
+        state_in[n] = jnp.zeros((E, K), jnp.float32)
+        for place in range(3):
+            def take(place=place):
+                for a, b, move in tails[n - 2]:
+                    if a == place:
+                        pl.when(rank[n - 2] == b)(move.wait_recv)
+                state = tails_in[n - 2, place]
+                if place:
+                    state = product(state_in[n], wide_in[n - 2, place - 1]) + state
+                state_in[n] = state * UP
+            pl.when(rank[n - 2] > place)(take)
+        return (product(state_in[n], prefix_ref[n]) + kept_ref[n]) * UP
+
+    rank = (gy, G - 1 - gy)
+
+    def member(way, place):
+        return at_y((place if way == 0 else G - 1 - place) * G + jy)
+
+    wholes = [
+        [(a, b, copy(whole_out.at[n], whole_in.at[n, a - 1], WY + 3 * n + q, member(n, b)))
+         for q, (a, b) in enumerate(WHOLE_PAIRS)]
+        for n in range(2)
+    ]
+    tails = [
+        [(a, b, copy(state_out.at[2 + n], tails_in.at[n, a], TY + 6 * n + q, member(n, b)))
+         for q, (a, b) in enumerate(TAIL_PAIRS)]
+        for n in range(2)
+    ]
     up, down = (0, 1, 2, 3), (3, 2, 1, 0)
     x_first, x_last = i < G, i >= NX_DEV - G
-    y_first, y_last = j < G, j >= NY_DEV - G
     step_xf = step_of(0, EXF, at_x(i + G))
     step_xb = step_of(1, EXB, at_x(i - G))
-    step_yf = step_of(2, EYF, at_y(j + G))
-    step_yb = step_of(3, EYB, at_y(j - G))
     early = i < NX_DEV // 2
     late = jnp.logical_not(early)
+    before = i < NX_DEV - 2 * G
 
     def receive_x(n):
         ops_x[n][1].wait_recv()
@@ -285,10 +318,23 @@
                 ops_y[n][d].wait_recv()
                 widen(got_y.at[n, d], wide_y.at[n, d + 1])
             compose(2 + n, wide_y, n, slot_y, order, jy)
+            for a, _, move in wholes[n]:
+                pl.when(rank[n] == a)(move.start)
+        for n in range(2):
+            for a, b, move in wholes[n]:
+                def take(a=a, move=move, n=n):
+                    move.wait_recv()
+                    widen(whole_in.at[n, a - 1], wide_in.at[n, a - 1])
+                pl.when(rank[n] == b)(take)
 
     moves_sx = share(0, SX, [at_x(p) for p in xp])
     receive_x(0)
     inside(0, moves_sx, wide_x, 0, slot_x, up, ix, x_first, step_xf)
+    ops_x[1][1].start()
+    ops_x[1][0].start()
+    for n in range(2):
+        for move in ops_y[n]:
+            move.start()
     compose(0, wide_x, 0, slot_x, up, ix)
     pl.when(late)(ready_back_x)
     ahead = across_groups(0, x_first, x_last, step_xf)
@@ -296,7 +342,7 @@
     moves_qx = share(1, QX, [at_x(p) for p in xp])
     pl.when(early)(ready_back_x)
     inside(1, moves_qx, wide_x, 1, slot_x, down, ix, x_last, step_xb)
-    pl.when(early)(ready_y)
+    pl.when(before)(ready_y)
     across_ref[...] = across_groups(1, x_last, x_first, step_xb)
 
     def gather_y(e, _):
@@ -309,13 +355,13 @@
 
     lax.fori_loop(0, E, gather_y, 0)
     moves_sy = share(2, SY, [at_y(p) for p in yp])
-    pl.when(late)(ready_y)
-    inside(2, moves_sy, wide_y, 0, slot_y, up, jy, y_first, step_yf)
-    ahead = across_groups(2, y_first, y_last, step_yf)
+    pl.when(jnp.logical_not(before))(ready_y)
+    inside(2, moves_sy, wide_y, 0, slot_y, up, jy)
+    ahead = entry_y(2)
     src_ref[3, 0] = product(ahead, wide_c[1])
     moves_qy = share(3, QY, [at_y(p) for p in yp])
-    inside(3, moves_qy, wide_y, 1, slot_y, down, jy, y_last, step_yb)
-    along_ref[...] = across_groups(3, y_last, y_first, step_yb)
+    inside(3, moves_qy, wide_y, 1, slot_y, down, jy)
+    along_ref[...] = entry_y(3)
 
     def finish(e, _):
         t = jnp.where(mine, along_ref[pl.ds(e, 1), :], 0.0)
@@ -335,8 +381,9 @@
             move.wait_send()
     pl.when(jnp.logical_not(x_last))(step_xf.wait_send)
     pl.when(jnp.logical_not(x_first))(step_xb.wait_send)
-    pl.when(jnp.logical_not(y_last))(step_yf.wait_send)
-    pl.when(jnp.logical_not(y_first))(step_yb.wait_send)
+    for n in range(2):
+        for a, _, move in wholes[n] + tails[n]:
+            pl.when(rank[n] == a)(move.wait_send)
 
 
 def local(*arrays):
@@ -361,11 +408,15 @@
             pltpu.VMEM((2, K, 2 * K), bf16),
             pltpu.VMEM((4, K, 2 * K), bf16),
             pltpu.VMEM((4, K, 2 * K), bf16),
+            pltpu.VMEM((2, K, K), f32),
+            pltpu.VMEM((2, 2, K, K), f32),
+            pltpu.VMEM((2, 2, K, 2 * K), bf16),
             pltpu.VMEM((4, G, E, K), f32),
             pltpu.VMEM((4, E, K), f32),
             pltpu.VMEM((4, E, K), f32),
             pltpu.VMEM((4, E, K), f32),
             pltpu.VMEM((4, E, K), f32),
+            pltpu.VMEM((2, 3, E, K), f32),
             pltpu.VMEM((E, K), f32),
             pltpu.VMEM((E, K), f32),
             pltpu.SemaphoreType.DMA((COPIES,)),

time: 123 us -> 113 us (0.919)
  Pallas kernels: 111 us -> 99.8 us
    pallas_call x1, Pallas kernels: 111 us -> 99.8 us  [local(): pl.pallas_call(kernel, out_shape=jax.ShapeDtypeStruct((E, C, K), f32), in...]
where the time goes in v3:
time: 113 us; the launch traced here: 111 us
  Pallas kernels  99.8 us (88%)
  local copies, waits for them, and re-layouts  11.6 us (10%)
    pallas_call x1, Pallas kernels, local(): pl.pallas_call(kernel, out_shape=jax.ShapeDtypeStruct((E, C, K), f32), in...  99.8 us
    unnamed x27, local copies, waits for them, and re-layouts  11.6 us

profile of v3, /device:TPU:6, one launch (start us, length us, event | category | flops | bytes accessed | tf_op | source)
XLA Modules:
  0.0 111.4 jit_solution(1215970261795847290)
XLA Ops:
  0.0 0.0 copy-start
  0.0 0.9 copy-done
  1.0 0.0 copy-start.1
  1.0 0.9 copy-done.1
  1.9 0.0 copy-start.2
  1.9 0.9 copy-done.2
  2.9 0.0 copy-start.3
  2.9 0.9 copy-done.3
  3.8 0.0 copy-start.4
  3.8 0.9 copy-done.4
  4.8 0.0 copy-start.5
  4.8 0.9 copy-done.5
  5.7 0.0 copy-start.6
  5.7 0.9 copy-done.6
  6.7 0.0 copy-start.7
  6.7 0.7 copy-done.7
  7.4 0.0 copy-start.8
  7.4 0.7 copy-done.8
  8.1 0.7 copy-done.9
  8.8 0.7 copy-done.10
  9.5 0.7 copy-done.11
  10.2 0.7 copy-done.12
  10.9 99.8 %shard_map.127 = f32[16,16,256]{2,1,0:T(8,128)S(1)} custom-call(f32[16,16,256]{2,1,0:T(8,128)S(1)} %copy-done, s32[16,256]{1,0:T(8,128)S(1)} %copy-done.7, s32[16,256]{1,0:T(8,128)S(1)} %copy-done.8, f32[16,256]{1,0:T(8,128)S(1)} %copy-done.9, f32[8]{0:T(128)S(1)} %copy-done.12, f32[16,256]{1,0:T(8,128)S(1)} %copy-done.10, f32[16,256]{1,0:T(8,128)S(1)} %copy-done.11, ...), custom_call_target="tpu_custom_call" | custom-call | tf_op jit(solution)/shard_map/pallas_call | solution.py:393
  110.7 0.7 copy.15
  (4 shorter events, 0.0 us)
Async XLA Ops:
  0.0 0.9 copy-start
  1.0 0.9 copy-start.1
  1.9 0.9 copy-start.2
  2.9 0.9 copy-start.3
  3.8 0.9 copy-start.4
  4.8 0.9 copy-start.5
  5.7 0.9 copy-start.6
  6.7 0.7 copy-start.7
  7.4 0.7 copy-start.8
  8.1 0.7 copy-start.9
  8.8 0.7 copy-start.10
  9.5 0.7 copy-start.11
  10.2 0.7 copy-start.12

commit v4 on v3

--- a/solution.py
+++ b/solution.py
@@ -50,13 +50,23 @@
 
 def kernel(
     start_ref, classes_ref, conductor_ref, drive_ref, perm_ref, leaf_x_ref, leaf_y_ref,
-    fwd_x_ref, back_x_ref, couple_x_ref, fwd_y_ref, back_y_ref, couple_y_ref,
+    fwd_x_hbm, back_x_hbm, couple_x_hbm, fwd_y_hbm, back_y_hbm, couple_y_hbm,
     out_ref,
+    own_ref,
     edge_out, edge_in, row_in, resid_ref, permit_ref,
     got_x, got_y, wide_x, wide_y, wide_c, whole_ref, prefix_ref, whole_out, whole_in, wide_in,
     src_ref, kept_ref, tail_ref, state_out, state_in, tails_in, across_ref, along_ref,
-    send_sem, recv_sem,
+    send_sem, recv_sem, own_sem,
 ):
+    fetches = [
+        pltpu.make_async_copy(ref, own_ref.at[n], own_sem.at[n])
+        for n, ref in enumerate(
+            (fwd_x_hbm, couple_x_hbm, couple_y_hbm, back_x_hbm, fwd_y_hbm, back_y_hbm))
+    ]
+    for move in fetches:
+        move.start()
+    fwd_x_ref, couple_x_ref, couple_y_ref, back_x_ref, fwd_y_ref, back_y_ref = (
+        own_ref.at[n] for n in range(6))
     i = lax.axis_index("gx")
     j = lax.axis_index("gy")
     ix, gx = i % G, i // G
@@ -136,6 +146,7 @@
         ops_y.append([
             copy(ref, got_y.at[n, d], number + d, at_y(yp[d])) for d in range(3)
         ])
+    fetches[0].wait()
     ops_x[0][1].start()
     ops_x[0][0].start()
 
@@ -144,6 +155,8 @@
         target[:, :K] = high
         target[:, K:] = low
 
+    for move in fetches[1:]:
+        move.wait()
     widen(couple_x_ref, wide_c.at[0])
     widen(couple_y_ref, wide_c.at[1])
     widen(fwd_x_ref, wide_x.at[0, 0])
@@ -168,6 +181,14 @@
         def clear(target=target):
             target[...] = jnp.zeros(target.shape, jnp.float32)
         pl.when(jnp.logical_not(receives))(clear)
+
+    def by_four(body):
+        def four(q, _):
+            for r in range(4):
+                body(4 * q + r, 0)
+            return 0
+
+        lax.fori_loop(0, E // 4, four, 0)
 
     def residual(e, _):
         x = start_ref[e]
@@ -190,7 +211,7 @@
         src_ref[0, 0, pl.ds(e, 1), :] = jnp.sum(leaf_x_ref[...] * resid, axis=0, keepdims=True)
         return 0
 
-    lax.fori_loop(0, E, residual, 0)
+    by_four(residual)
 
     def share(n, number, places):
         moves = [
@@ -353,7 +374,7 @@
         src_ref[2, 0, pl.ds(e, 1), :] = jnp.sum(jnp.where(mine, t, 0.0), axis=0, keepdims=True)
         return 0
 
-    lax.fori_loop(0, E, gather_y, 0)
+    by_four(gather_y)
     moves_sy = share(2, SY, [at_y(p) for p in yp])
     pl.when(jnp.logical_not(before))(ready_y)
     inside(2, moves_sy, wide_y, 0, slot_y, up, jy)
@@ -372,7 +393,7 @@
         )
         return 0
 
-    lax.fori_loop(0, E, finish, 0)
+    by_four(finish)
 
     for sends, _, move in halo:
         pl.when(sends)(move.wait_send)
@@ -389,13 +410,15 @@
 def local(*arrays):
     vmem = pl.BlockSpec(memory_space=pltpu.VMEM)
     smem = pl.BlockSpec(memory_space=pltpu.SMEM)
+    hbm = pl.BlockSpec(memory_space=pl.ANY)
     f32, bf16 = jnp.float32, jnp.bfloat16
     return pl.pallas_call(
         kernel,
         out_shape=jax.ShapeDtypeStruct((E, C, K), f32),
-        in_specs=[vmem] * 4 + [smem] + [vmem] * 8,
+        in_specs=[vmem] * 4 + [smem] + [vmem] * 2 + [hbm] * 6,
         out_specs=vmem,
         scratch_shapes=[
+            pltpu.VMEM((6, K, K), f32),
             pltpu.VMEM((2, E, K), f32),
             pltpu.VMEM((2, E, K), f32),
             pltpu.VMEM((2, E, C, K // 2), f32),
@@ -421,6 +444,7 @@
             pltpu.VMEM((E, K), f32),
             pltpu.SemaphoreType.DMA((COPIES,)),
             pltpu.SemaphoreType.DMA((COPIES,)),
+            pltpu.SemaphoreType.DMA((6,)),
         ],
         compiler_params=pltpu.CompilerParams(
             collective_id=0, has_side_effects=True, vmem_limit_bytes=48 * 1024 * 1024

time: 113 us -> 108 us (0.956)
  Pallas kernels: 99.8 us -> 94.9 us
    pallas_call x1, Pallas kernels: 99.8 us -> 94.9 us  [local(): pl.pallas_call(kernel, out_shape=jax.ShapeDtypeStruct((E, C, K), f32), in...]
where the time goes in v4:
time: 108 us; the launch traced here: 107 us
  Pallas kernels  94.9 us (88%)
  local copies, waits for them, and re-layouts  11.6 us (11%)
    pallas_call x1, Pallas kernels, local(): pl.pallas_call(kernel, out_shape=jax.ShapeDtypeStruct((E, C, K), f32), in...  94.9 us
    unnamed x27, local copies, waits for them, and re-layouts  11.6 us

profile of v4, /device:TPU:6, one launch (start us, length us, event | category | flops | bytes accessed | tf_op | source)
XLA Modules:
  0.0 106.5 jit_solution(316907572546015586)
XLA Ops:
  0.0 0.0 copy-start
  0.0 0.9 copy-done
  1.0 0.0 copy-start.1
  1.0 0.9 copy-done.1
  1.9 0.0 copy-start.2
  1.9 0.9 copy-done.2
  2.9 0.0 copy-start.3
  2.9 0.9 copy-done.3
  3.8 0.0 copy-start.4
  3.8 0.9 copy-done.4
  4.8 0.0 copy-start.5
  4.8 0.9 copy-done.5
  5.7 0.0 copy-start.6
  5.7 0.9 copy-done.6
  6.7 0.0 copy-start.7
  6.7 0.7 copy-done.7
  7.4 0.0 copy-start.8
  7.4 0.7 copy-done.8
  8.1 0.7 copy-done.9
  8.8 0.7 copy-done.10
  9.5 0.7 copy-done.11
  10.2 0.7 copy-done.12
  10.9 94.9 %shard_map.127 = f32[16,16,256]{2,1,0:T(8,128)S(1)} custom-call(f32[16,16,256]{2,1,0:T(8,128)S(1)} %copy-done, s32[16,256]{1,0:T(8,128)S(1)} %copy-done.7, s32[16,256]{1,0:T(8,128)S(1)} %copy-done.8, f32[16,256]{1,0:T(8,128)S(1)} %copy-done.9, f32[8]{0:T(128)S(1)} %copy-done.12, f32[16,256]{1,0:T(8,128)S(1)} %copy-done.10, f32[16,256]{1,0:T(8,128)S(1)} %copy-done.11, ...), custom_call_target="tpu_custom_call" | custom-call | tf_op jit(solution)/shard_map/pallas_call | solution.py:415
  105.8 0.7 copy.15
  (4 shorter events, 0.0 us)
Async XLA Ops:
  0.0 0.9 copy-start
  1.0 0.9 copy-start.1
  1.9 0.9 copy-start.2
  2.9 0.9 copy-start.3
  3.8 0.9 copy-start.4
  4.8 0.9 copy-start.5
  5.7 0.9 copy-start.6
  6.7 0.7 copy-start.7
  7.4 0.7 copy-start.8
  8.1 0.7 copy-start.9
  8.8 0.7 copy-start.10
  9.5 0.7 copy-start.11
  10.2 0.7 copy-start.12

commit v5 on v4

--- a/solution.py
+++ b/solution.py
@@ -22,7 +22,8 @@
 EXF, EXB = 28, 29
 WY = 30
 TY = 36
-COPIES = 48
+EXB_NEAR, TX, WX = 48, 49, 50
+COPIES = 51
 WHOLE_PAIRS = ((1, 2), (1, 3), (2, 3))
 TAIL_PAIRS = ((0, 1), (0, 2), (0, 3), (1, 2), (1, 3), (2, 3))
 
@@ -52,7 +53,7 @@
     start_ref, classes_ref, conductor_ref, drive_ref, perm_ref, leaf_x_ref, leaf_y_ref,
     fwd_x_hbm, back_x_hbm, couple_x_hbm, fwd_y_hbm, back_y_hbm, couple_y_hbm,
     out_ref,
-    own_ref,
+    own_ref, tail_x_in, wide_x_in,
     edge_out, edge_in, row_in, resid_ref, permit_ref,
     got_x, got_y, wide_x, wide_y, wide_c, whole_ref, prefix_ref, whole_out, whole_in, wide_in,
     src_ref, kept_ref, tail_ref, state_out, state_in, tails_in, across_ref, along_ref,
@@ -99,6 +100,8 @@
         ((ix == G - 1) & (i < NX_DEV - 1), at_x(i + 1)),
         (i >= G, at_x(i - G)),
         (i < NX_DEV - G, at_x(i + G)),
+        ((gx % 2 == 0) & (gx >= 2), at_x(i - 2 * G)),
+        ((gx % 2 == 0) & (gx <= 4), at_x(i + 2 * G)),
         ((jy == 0) & (j > 0), at_y(j - 1)),
         ((jy == G - 1) & (j < NY_DEV - 1), at_y(j + 1)),
     ]
@@ -240,8 +243,8 @@
                 pl.when(position == k)(functools.partial(put, prefix_ref, x))
                 high, low = split(x)
             put(whole_ref, x)
-            if n >= 2:
-                whole_out[n - 2, rows, :] = x * DOWN
+            if n >= 1:
+                whole_out[(n + 1) % 3, rows, :] = x * DOWN
             return 0
 
         lax.fori_loop(0, K // ROWS, part, 0)
@@ -259,6 +262,18 @@
             state = product(state, wide[way, s]) + src_ref[n, s] * DOWN
             kept = jnp.where(position == k, state, kept)
         kept_ref[n] = kept
+        if n == 1:
+            tail_ref[n] = state
+
+            def pass_tail():
+                state_out[n] = state
+                tail_x.start()
+            pl.when(odd)(pass_tail)
+
+            def clear():
+                state_in[n] = jnp.zeros((E, K), jnp.float32)
+            pl.when(gx >= 6)(clear)
+            return
         if step is None:
             state_out[n] = state
             for a, _, move in tails[n - 2]:
@@ -315,7 +330,36 @@
     up, down = (0, 1, 2, 3), (3, 2, 1, 0)
     x_first, x_last = i < G, i >= NX_DEV - G
     step_xf = step_of(0, EXF, at_x(i + G))
-    step_xb = step_of(1, EXB, at_x(i - G))
+    odd = gx % 2 == 1
+    even = jnp.logical_not(odd)
+    far = step_of(1, EXB, at_x(i - 2 * G))
+    near = step_of(1, EXB_NEAR, at_x(i - G))
+    tail_x = copy(state_out.at[1], tail_x_in, TX, at_x(i - G))
+    whole_x = copy(whole_out.at[2], whole_in.at[2, 0], WX, at_x(i - G))
+
+    def entry_back_x():
+        pl.when(odd & (gx < 6))(near.wait_recv)
+
+        def pair():
+            pl.when(gx < 6)(far.wait_recv)
+            tail_x.wait_recv()
+
+            def through():
+                state_in[1] = (product(state_in[1], wide_x_in[...]) + tail_x_in[...]) * UP
+            pl.when(gx < 6)(through)
+
+            def only():
+                state_in[1] = tail_x_in[...] * UP
+            pl.when(gx >= 6)(only)
+
+            def give():
+                state_out[1] = (product(state_in[1], whole_ref[1]) + tail_ref[1]) * UP
+                far.start()
+                near.start()
+            pl.when(gx >= 2)(give)
+        pl.when(even)(pair)
+        return (product(state_in[1], prefix_ref[1]) + kept_ref[1]) * UP
+
     early = i < NX_DEV // 2
     late = jnp.logical_not(early)
     before = i < NX_DEV - 2 * G
@@ -332,6 +376,7 @@
     def ready_back_x():
         receive_x(1)
         compose(1, wide_x, 1, slot_x, down, ix)
+        pl.when(odd & (gx < 6))(whole_x.start)
 
     def ready_y():
         for n, order in ((0, up), (1, down)):
@@ -362,9 +407,14 @@
     src_ref[1, 0] = product(ahead, wide_c[0])
     moves_qx = share(1, QX, [at_x(p) for p in xp])
     pl.when(early)(ready_back_x)
-    inside(1, moves_qx, wide_x, 1, slot_x, down, ix, x_last, step_xb)
+    inside(1, moves_qx, wide_x, 1, slot_x, down, ix)
+
+    def take_whole_x():
+        whole_x.wait_recv()
+        widen(whole_in.at[2, 0], wide_x_in)
+    pl.when(even & (gx < 6))(take_whole_x)
     pl.when(before)(ready_y)
-    across_ref[...] = across_groups(1, x_last, x_first, step_xb)
+    across_ref[...] = entry_back_x()
 
     def gather_y(e, _):
         lifted = resid_ref[e] + leaf_x_ref[...] * across_ref[pl.ds(e, 1), :]
@@ -401,7 +451,10 @@
         for move in moves:
             move.wait_send()
     pl.when(jnp.logical_not(x_last))(step_xf.wait_send)
-    pl.when(jnp.logical_not(x_first))(step_xb.wait_send)
+    for move in (far, near):
+        pl.when(even & (gx >= 2))(move.wait_send)
+    pl.when(odd)(tail_x.wait_send)
+    pl.when(odd & (gx < 6))(whole_x.wait_send)
     for n in range(2):
         for a, _, move in wholes[n] + tails[n]:
             pl.when(rank[n] == a)(move.wait_send)
@@ -419,6 +472,8 @@
         out_specs=vmem,
         scratch_shapes=[
             pltpu.VMEM((6, K, K), f32),
+            pltpu.VMEM((E, K), f32),
+            pltpu.VMEM((K, 2 * K), bf16),
             pltpu.VMEM((2, E, K), f32),
             pltpu.VMEM((2, E, K), f32),
             pltpu.VMEM((2, E, C, K // 2), f32),
@@ -431,8 +486,8 @@
             pltpu.VMEM((2, K, 2 * K), bf16),
             pltpu.VMEM((4, K, 2 * K), bf16),
             pltpu.VMEM((4, K, 2 * K), bf16),
-            pltpu.VMEM((2, K, K), f32),
-            pltpu.VMEM((2, 2, K, K), f32),
+            pltpu.VMEM((3, K, K), f32),
+            pltpu.VMEM((3, 2, K, K), f32),
             pltpu.VMEM((2, 2, K, 2 * K), bf16),
             pltpu.VMEM((4, G, E, K), f32),
             pltpu.VMEM((4, E, K), f32),
@@ -447,7 +502,7 @@
             pltpu.SemaphoreType.DMA((6,)),
         ],
         compiler_params=pltpu.CompilerParams(
-            collective_id=0, has_side_effects=True, vmem_limit_bytes=48 * 1024 * 1024
+            collective_id=0, has_side_effects=True, vmem_limit_bytes=63 * 1024 * 1024
         ),
     )(*arrays)
 

time: 108 us -> 95.8 us (0.89)
  local copies, waits for them, and re-layouts: 11.6 us -> 1.67 us
  Pallas kernels: 94.9 us -> 93.5 us
    unnamed x27 -> x1, local copies, waits for them, and re-layouts: 11.6 us -> 1.67 us
    pallas_call x1, Pallas kernels: 94.9 us -> 93.5 us  [local(): pl.pallas_call(kernel, out_shape=jax.ShapeDtypeStruct((E, C, K), f32), in...]
where the time goes in v5:
time: 95.8 us; the launch traced here: 95.2 us
  Pallas kernels  93.5 us (98%)
  local copies, waits for them, and re-layouts  1.67 us (2%)
    pallas_call x1, Pallas kernels, local(): pl.pallas_call(kernel, out_shape=jax.ShapeDtypeStruct((E, C, K), f32), in...  93.5 us

profile of v5, /device:TPU:6, one launch (start us, length us, event | category | flops | bytes accessed | tf_op | source)
XLA Modules:
  0.0 95.2 jit_solution(2132886251066626074)
XLA Ops:
  0.0 93.5 %shard_map.127 = f32[16,16,256]{2,1,0:T(8,128)} custom-call(f32[16,16,256]{2,1,0:T(8,128)} %start_ref.1, s32[16,256]{1,0:T(8,128)} %classes_ref.1, s32[16,256]{1,0:T(8,128)} %conductor_ref.1, f32[16,256]{1,0:T(8,128)} %drive_ref.1, f32[8]{0:T(128)} %perm_ref.1, f32[16,256]{1,0:T(8,128)} %leaf_x_ref.1, f32[16,256]{1,0:T(8,128)} %leaf_y_ref.1, ...), custom_call_target="tpu_custom_call" | custom-call | tf_op jit(solution)/shard_map/pallas_call | solution.py:468
  93.5 1.7 %copy.15 = f32[16,16,256]{2,1,0:T(8,128)} copy(f32[16,16,256]{2,1,0:T(8,128)} %shard_map.127) | data formatting | bytes 524288

commit v6 on v5

--- a/solution.py
+++ b/solution.py
@@ -23,7 +23,8 @@
 WY = 30
 TY = 36
 EXB_NEAR, TX, WX = 48, 49, 50
-COPIES = 51
+EXF_FAR, TXF, WXF = 51, 52, 53
+COPIES = 54
 WHOLE_PAIRS = ((1, 2), (1, 3), (2, 3))
 TAIL_PAIRS = ((0, 1), (0, 2), (0, 3), (1, 2), (1, 3), (2, 3))
 
@@ -50,10 +51,11 @@
 
 
 def kernel(
-    start_ref, classes_ref, conductor_ref, drive_ref, perm_ref, leaf_x_ref, leaf_y_ref,
+    start_hbm, classes_hbm, conductor_hbm, drive_hbm, perm_ref, leaf_x_hbm, leaf_y_hbm,
     fwd_x_hbm, back_x_hbm, couple_x_hbm, fwd_y_hbm, back_y_hbm, couple_y_hbm,
     out_ref,
-    own_ref, tail_x_in, wide_x_in,
+    own_ref, tail_x_in, wide_x_in, tail_f_in, wide_f_in,
+    start_ref, classes_ref, conductor_ref, drive_ref, leaf_x_ref, leaf_y_ref,
     edge_out, edge_in, row_in, resid_ref, permit_ref,
     got_x, got_y, wide_x, wide_y, wide_c, whole_ref, prefix_ref, whole_out, whole_in, wide_in,
     src_ref, kept_ref, tail_ref, state_out, state_in, tails_in, across_ref, along_ref,
@@ -64,8 +66,12 @@
         for n, ref in enumerate(
             (fwd_x_hbm, couple_x_hbm, couple_y_hbm, back_x_hbm, fwd_y_hbm, back_y_hbm))
     ]
-    for move in fetches:
-        move.start()
+    cells = [
+        pltpu.make_async_copy(src, dst, own_sem.at[6 + n])
+        for n, (src, dst) in enumerate((
+            (start_hbm, start_ref), (classes_hbm, classes_ref), (conductor_hbm, conductor_ref),
+            (drive_hbm, drive_ref), (leaf_x_hbm, leaf_x_ref), (leaf_y_hbm, leaf_y_ref)))
+    ]
     fwd_x_ref, couple_x_ref, couple_y_ref, back_x_ref, fwd_y_ref, back_y_ref = (
         own_ref.at[n] for n in range(6))
     i = lax.axis_index("gx")
@@ -100,8 +106,8 @@
         ((ix == G - 1) & (i < NX_DEV - 1), at_x(i + 1)),
         (i >= G, at_x(i - G)),
         (i < NX_DEV - G, at_x(i + G)),
-        ((gx % 2 == 0) & (gx >= 2), at_x(i - 2 * G)),
-        ((gx % 2 == 0) & (gx <= 4), at_x(i + 2 * G)),
+        (((gx % 2 == 0) & (gx >= 2)) | (gx == 5) | (gx == 7), at_x(i - 2 * G)),
+        (((gx % 2 == 0) & (gx <= 4)) | (gx == 3) | (gx == 5), at_x(i + 2 * G)),
         ((jy == 0) & (j > 0), at_y(j - 1)),
         ((jy == G - 1) & (j < NY_DEV - 1), at_y(j + 1)),
     ]
@@ -113,6 +119,9 @@
             greet()
         else:
             pl.when(held)(greet)
+    for move in cells + fetches:
+        move.start()
+    cells[0].wait()
     edge_out[0] = start_ref[:, C - 1, :]
     edge_out[1] = start_ref[:, 0, :]
     count = 9
@@ -158,7 +167,7 @@
         target[:, :K] = high
         target[:, K:] = low
 
-    for move in fetches[1:]:
+    for move in fetches[1:] + cells[1:]:
         move.wait()
     widen(couple_x_ref, wide_c.at[0])
     widen(couple_y_ref, wide_c.at[1])
@@ -243,8 +252,7 @@
                 pl.when(position == k)(functools.partial(put, prefix_ref, x))
                 high, low = split(x)
             put(whole_ref, x)
-            if n >= 1:
-                whole_out[(n + 1) % 3, rows, :] = x * DOWN
+            whole_out[(3, 2, 0, 1)[n], rows, :] = x * DOWN
             return 0
 
         lax.fori_loop(0, K // ROWS, part, 0)
@@ -287,16 +295,29 @@
             state_in[n] = jnp.zeros((E, K), jnp.float32)
         pl.when(first)(begin)
 
-    def across_groups(n, first, last, step):
-        def take():
-            step.wait_recv()
-        pl.when(jnp.logical_not(first))(take)
+        def pass_on():
+            state_out[n] = state
+            tail_f.start()
+        pl.when((gx == 4) | (gx == 6))(pass_on)
+
+    def entry_fwd_x():
+        step = step_xf
+        pl.when(((gx >= 1) & (gx <= 4)) | (gx == 6))(step.wait_recv)
+
+        def pair():
+            whole_f.wait_recv()
+            widen(whole_in.at[3, 0], wide_f_in)
+            tail_f.wait_recv()
+            far_f.wait_recv()
+            state_in[0] = (product(state_in[0], wide_f_in[...]) + tail_f_in[...]) * UP
+        pl.when((gx == 5) | (gx == 7))(pair)
 
         def give():
-            state_out[n] = (product(state_in[n], whole_ref[n]) + tail_ref[n]) * UP
+            state_out[0] = (product(state_in[0], whole_ref[0]) + tail_ref[0]) * UP
+            pl.when((gx == 3) | (gx == 5))(far_f.start)
             step.start()
-        pl.when(jnp.logical_not(first) & jnp.logical_not(last))(give)
-        return (product(state_in[n], prefix_ref[n]) + kept_ref[n]) * UP
+        pl.when(((gx >= 1) & (gx <= 3)) | (gx == 5))(give)
+        return (product(state_in[0], prefix_ref[0]) + kept_ref[0]) * UP
 
     def entry_y(n):
         state_in[n] = jnp.zeros((E, K), jnp.float32)
@@ -328,8 +349,11 @@
         for n in range(2)
     ]
     up, down = (0, 1, 2, 3), (3, 2, 1, 0)
-    x_first, x_last = i < G, i >= NX_DEV - G
+    x_first = i < G
     step_xf = step_of(0, EXF, at_x(i + G))
+    far_f = step_of(0, EXF_FAR, at_x(i + 2 * G))
+    tail_f = copy(state_out.at[0], tail_f_in, TXF, at_x(i + G))
+    whole_f = copy(whole_out.at[3], whole_in.at[3, 0], WXF, at_x(i + G))
     odd = gx % 2 == 1
     even = jnp.logical_not(odd)
     far = step_of(1, EXB, at_x(i - 2 * G))
@@ -402,8 +426,9 @@
         for move in ops_y[n]:
             move.start()
     compose(0, wide_x, 0, slot_x, up, ix)
+    pl.when((gx == 4) | (gx == 6))(whole_f.start)
     pl.when(late)(ready_back_x)
-    ahead = across_groups(0, x_first, x_last, step_xf)
+    ahead = entry_fwd_x()
     src_ref[1, 0] = product(ahead, wide_c[0])
     moves_qx = share(1, QX, [at_x(p) for p in xp])
     pl.when(early)(ready_back_x)
@@ -450,7 +475,10 @@
     for moves in ops_x + ops_y + [moves_sx, moves_qx, moves_sy, moves_qy]:
         for move in moves:
             move.wait_send()
-    pl.when(jnp.logical_not(x_last))(step_xf.wait_send)
+    pl.when((gx <= 3) | (gx == 5))(step_xf.wait_send)
+    pl.when((gx == 3) | (gx == 5))(far_f.wait_send)
+    for move in (tail_f, whole_f):
+        pl.when((gx == 4) | (gx == 6))(move.wait_send)
     for move in (far, near):
         pl.when(even & (gx >= 2))(move.wait_send)
     pl.when(odd)(tail_x.wait_send)
@@ -468,12 +496,20 @@
     return pl.pallas_call(
         kernel,
         out_shape=jax.ShapeDtypeStruct((E, C, K), f32),
-        in_specs=[vmem] * 4 + [smem] + [vmem] * 2 + [hbm] * 6,
+        in_specs=[hbm] * 4 + [smem] + [hbm] * 8,
         out_specs=vmem,
         scratch_shapes=[
             pltpu.VMEM((6, K, K), f32),
             pltpu.VMEM((E, K), f32),
             pltpu.VMEM((K, 2 * K), bf16),
+            pltpu.VMEM((E, K), f32),
+            pltpu.VMEM((K, 2 * K), bf16),
+            pltpu.VMEM((E, C, K), f32),
+            pltpu.VMEM((C, K), jnp.int32),
+            pltpu.VMEM((C, K), jnp.int32),
+            pltpu.VMEM((C, K), f32),
+            pltpu.VMEM((C, K), f32),
+            pltpu.VMEM((C, K), f32),
             pltpu.VMEM((2, E, K), f32),
             pltpu.VMEM((2, E, K), f32),
             pltpu.VMEM((2, E, C, K // 2), f32),
@@ -486,8 +522,8 @@
             pltpu.VMEM((2, K, 2 * K), bf16),
             pltpu.VMEM((4, K, 2 * K), bf16),
             pltpu.VMEM((4, K, 2 * K), bf16),
-            pltpu.VMEM((3, K, K), f32),
-            pltpu.VMEM((3, 2, K, K), f32),
+            pltpu.VMEM((4, K, K), f32),
+            pltpu.VMEM((4, 2, K, K), f32),
             pltpu.VMEM((2, 2, K, 2 * K), bf16),
             pltpu.VMEM((4, G, E, K), f32),
             pltpu.VMEM((4, E, K), f32),
@@ -499,7 +535,7 @@
             pltpu.VMEM((E, K), f32),
             pltpu.SemaphoreType.DMA((COPIES,)),
             pltpu.SemaphoreType.DMA((COPIES,)),
-            pltpu.SemaphoreType.DMA((6,)),
+            pltpu.SemaphoreType.DMA((12,)),
         ],
         compiler_params=pltpu.CompilerParams(
             collective_id=0, has_side_effects=True, vmem_limit_bytes=63 * 1024 * 1024

time: 95.8 us -> 95.6 us (level)
  the two profiles are of different devices: /device:TPU:6 before, /device:TPU:32 now
where the time goes in v6:
time: 95.6 us; the launch traced here: 95.4 us
  Pallas kernels  93.7 us (98%)
  local copies, waits for them, and re-layouts  1.67 us (2%)
    pallas_call x1, Pallas kernels, local(): pl.pallas_call(kernel, out_shape=jax.ShapeDtypeStruct((E, C, K), f32), in...  93.7 us

profile of v6, /device:TPU:32, one launch (start us, length us, event | category | flops | bytes accessed | tf_op | source)
XLA Modules:
  0.0 95.4 jit_solution(6059029949716315158)
XLA Ops:
  0.0 93.7 %shard_map.127 = f32[16,16,256]{2,1,0:T(8,128)} custom-call(f32[16,16,256]{2,1,0:T(8,128)} %start_hbm.1, s32[16,256]{1,0:T(8,128)} %classes_hbm.1, s32[16,256]{1,0:T(8,128)} %conductor_hbm.1, f32[16,256]{1,0:T(8,128)} %drive_hbm.1, f32[8]{0:T(128)} %perm_ref.1, f32[16,256]{1,0:T(8,128)} %leaf_x_hbm.1, f32[16,256]{1,0:T(8,128)} %leaf_y_hbm.1, ...), custom_call_target="tpu_custom_call" | custom-call | tf_op jit(solution)/shard_map/pallas_call | solution.py:496
  93.7 1.7 %copy.15 = f32[16,16,256]{2,1,0:T(8,128)} copy(f32[16,16,256]{2,1,0:T(8,128)} %shard_map.127) | data formatting | bytes 524288

commit v7 on v5

--- a/solution.py
+++ b/solution.py
@@ -50,10 +50,11 @@
 
 
 def kernel(
-    start_ref, classes_ref, conductor_ref, drive_ref, perm_ref, leaf_x_ref, leaf_y_ref,
+    start_hbm, classes_hbm, conductor_hbm, drive_hbm, perm_ref, leaf_x_hbm, leaf_y_hbm,
     fwd_x_hbm, back_x_hbm, couple_x_hbm, fwd_y_hbm, back_y_hbm, couple_y_hbm,
     out_ref,
     own_ref, tail_x_in, wide_x_in,
+    start_ref, classes_ref, conductor_ref, drive_ref, leaf_x_ref, leaf_y_ref,
     edge_out, edge_in, row_in, resid_ref, permit_ref,
     got_x, got_y, wide_x, wide_y, wide_c, whole_ref, prefix_ref, whole_out, whole_in, wide_in,
     src_ref, kept_ref, tail_ref, state_out, state_in, tails_in, across_ref, along_ref,
@@ -64,8 +65,12 @@
         for n, ref in enumerate(
             (fwd_x_hbm, couple_x_hbm, couple_y_hbm, back_x_hbm, fwd_y_hbm, back_y_hbm))
     ]
-    for move in fetches:
-        move.start()
+    cells = [
+        pltpu.make_async_copy(src, dst, own_sem.at[6 + n])
+        for n, (src, dst) in enumerate((
+            (start_hbm, start_ref), (classes_hbm, classes_ref), (conductor_hbm, conductor_ref),
+            (drive_hbm, drive_ref), (leaf_x_hbm, leaf_x_ref), (leaf_y_hbm, leaf_y_ref)))
+    ]
     fwd_x_ref, couple_x_ref, couple_y_ref, back_x_ref, fwd_y_ref, back_y_ref = (
         own_ref.at[n] for n in range(6))
     i = lax.axis_index("gx")
@@ -113,6 +118,9 @@
             greet()
         else:
             pl.when(held)(greet)
+    for move in cells[:1] + fetches[:1] + cells[1:] + fetches[1:]:
+        move.start()
+    cells[0].wait()
     edge_out[0] = start_ref[:, C - 1, :]
     edge_out[1] = start_ref[:, 0, :]
     count = 9
@@ -158,7 +166,7 @@
         target[:, :K] = high
         target[:, K:] = low
 
-    for move in fetches[1:]:
+    for move in fetches[1:] + cells[1:]:
         move.wait()
     widen(couple_x_ref, wide_c.at[0])
     widen(couple_y_ref, wide_c.at[1])
@@ -468,12 +476,18 @@
     return pl.pallas_call(
         kernel,
         out_shape=jax.ShapeDtypeStruct((E, C, K), f32),
-        in_specs=[vmem] * 4 + [smem] + [vmem] * 2 + [hbm] * 6,
+        in_specs=[hbm] * 4 + [smem] + [hbm] * 8,
         out_specs=vmem,
         scratch_shapes=[
             pltpu.VMEM((6, K, K), f32),
             pltpu.VMEM((E, K), f32),
             pltpu.VMEM((K, 2 * K), bf16),
+            pltpu.VMEM((E, C, K), f32),
+            pltpu.VMEM((C, K), jnp.int32),
+            pltpu.VMEM((C, K), jnp.int32),
+            pltpu.VMEM((C, K), f32),
+            pltpu.VMEM((C, K), f32),
+            pltpu.VMEM((C, K), f32),
             pltpu.VMEM((2, E, K), f32),
             pltpu.VMEM((2, E, K), f32),
             pltpu.VMEM((2, E, C, K // 2), f32),
@@ -499,7 +513,7 @@
             pltpu.VMEM((E, K), f32),
             pltpu.SemaphoreType.DMA((COPIES,)),
             pltpu.SemaphoreType.DMA((COPIES,)),
-            pltpu.SemaphoreType.DMA((6,)),
+            pltpu.SemaphoreType.DMA((12,)),
         ],
         compiler_params=pltpu.CompilerParams(
             collective_id=0, has_side_effects=True, vmem_limit_bytes=63 * 1024 * 1024

time: 95.8 us -> 95.6 us (level)
  no operation moved by 1% of the time
where the time goes in v7:
time: 95.6 us; the launch traced here: 94.9 us
  Pallas kernels  93.2 us (97%)
  local copies, waits for them, and re-layouts  1.67 us (2%)
    pallas_call x1, Pallas kernels, local(): pl.pallas_call(kernel, out_shape=jax.ShapeDtypeStruct((E, C, K), f32), in...  93.2 us

profile of v7, /device:TPU:6, one launch (start us, length us, event | category | flops | bytes accessed | tf_op | source)
XLA Modules:
  0.0 94.9 jit_solution(12770251605217980239)
XLA Ops:
  0.0 93.2 %shard_map.127 = f32[16,16,256]{2,1,0:T(8,128)} custom-call(f32[16,16,256]{2,1,0:T(8,128)} %start_hbm.1, s32[16,256]{1,0:T(8,128)} %classes_hbm.1, s32[16,256]{1,0:T(8,128)} %conductor_hbm.1, f32[16,256]{1,0:T(8,128)} %drive_hbm.1, f32[8]{0:T(128)} %perm_ref.1, f32[16,256]{1,0:T(8,128)} %leaf_x_hbm.1, f32[16,256]{1,0:T(8,128)} %leaf_y_hbm.1, ...), custom_call_target="tpu_custom_call" | custom-call | tf_op jit(solution)/shard_map/pallas_call | solution.py:476
  93.2 1.7 %copy.15 = f32[16,16,256]{2,1,0:T(8,128)} copy(f32[16,16,256]{2,1,0:T(8,128)} %shard_map.127) | data formatting | bytes 524288
